TPU v7x, 32 devices: a whole 2x2x4 slice. The times are simulated.
32 devices in a mesh: groups: 2 (over x), elec: 8 (over z, y), walk: 2 (over core).
Axes of the slice: x: 2, y: 2, z: 4, core: 2. Of those that a mesh axis runs over, the one named last changes fastest.
Arguments:
- hidden: bfloat16 [16, 128, 256], P(('groups', 'walk'), 'elec'), parts along dimension 0, may hold values from -6 to 6
- cotangent: bfloat16 [16, 128, 256], P(('groups', 'walk'), 'elec'), parts along dimension 0, may hold values from -6 to 6
- positions: float32 [16, 3, 128], P(('groups', 'walk'), None, 'elec'), parts along dimension 0, may hold values from 0 to 1
- spins: int32 [256], P(('groups', 'elec')), parts along dimension 0, may hold values from 0 to 1
- w_in: bfloat16 [256, 32], replicated, may hold values from -0.375 to 0.375
- w_pair: float32 [32, 32], replicated, may hold values from -1 to 1
- spin_bias: float32 [2, 32], replicated, may hold values from -3 to 3
- rates: float32 [32], replicated, may hold values from 1 to 100
- w_out: bfloat16 [32, 256], replicated, may hold values from -1 to 1
Outputs:
- hidden_grad: bfloat16 [16, 128, 256], P(('groups', 'walk'), 'elec'), parts along dimension 0
- w_in_grad: float32 [512, 32], P('groups'), parts along dimension 0
- w_pair_grad: float32 [64, 32], P('groups'), parts along dimension 0
- spin_bias_grad: float32 [4, 32], P('groups'), parts along dimension 0
- w_out_grad: float32 [64, 256], P('groups'), parts along dimension 0
There are 2 independent parts, one for each index of `groups`. A program takes and returns all parts, laid end to end along the dimension named above; an argument that names none is the same for every part. Nothing has to cross between parts.
All inputs are finite; a program needn't handle non-finite values.
Results may differ from a plain program's by a relative error of at most 0.001.
Values sent between devices are 32-bit elements; how exact they have to be, the bound alone decides.
No kernel may reach another device: no remote copies, remote signals or barrier semaphores. Data moves between devices by JAX's collectives and lax.ppermute only.
A program may use at most 64 MiB of HBM per device.

v0:
```python
import functools

import jax
import jax.numpy as jnp
from jax import lax
from jax.experimental import pallas as pl
from jax.experimental.pallas import tpu as pltpu
from jax.sharding import PartitionSpec as P


F32, BF16 = jnp.float32, jnp.bfloat16
LANES = 128
PACK = 8


def dot(a, b, dims=((1,), (0,))):
    return lax.dot_general(a, b, (dims, ((), ())), preferred_element_type=F32)


def dot_exact(a, b, dims=((1,), (0,))):
    return lax.dot_general(
        a, b, (dims, ((), ())), precision=lax.Precision.HIGHEST, preferred_element_type=F32
    )


def split(x):
    high = x.astype(BF16)
    return high, (x - high.astype(F32)).astype(BF16)


def iota(shape, axis):
    return lax.broadcasted_iota(jnp.int32, shape, axis)


def flag(condition):
    return jnp.where(condition, 1.0, 0.0).astype(F32)


def embed_kernel(total, hid, cot, pos, spin, w_in, w_out, w_pair, spin_bias, rates, out, big_out, *copies):
    walkers, rows, hidden_width = hid.shape
    proj, sense = [], []
    block = 2 * rows + 8
    n_rows = walkers * rows
    for w in range(walkers):
        proj.append(dot(hid[w], w_in[...], ((1,), (1,))))
        sense.append(dot(cot[w], w_out[...], ((1,), (1,))) / total)
        for k in range(hidden_width // LANES):
            at = block + k * n_rows + w * rows
            big_out[at : at + rows] = hid[w][:, k * LANES : (k + 1) * LANES].astype(F32)
            at = at + hidden_width // LANES * n_rows
            big_out[at : at + rows] = cot[w][:, k * LANES : (k + 1) * LANES].astype(F32)
    feats = []
    for c in range(3):
        x = pos[c]
        feats.append(jnp.cos(jnp.concatenate([x, x - 0.25], axis=0) * (2.0 * jnp.pi)))
    labels = jnp.broadcast_to(spin[...].astype(F32), (8, rows))
    feats.append(jnp.where(iota((8, rows), 0) == 0, labels, 1.0))
    feat = jnp.concatenate(feats, axis=0).T
    parts = [feat[8 * k : 8 * k + 8] for k in range(rows // 8)]
    parts.append(jnp.zeros((8, LANES - feat.shape[1] * (rows // 8)), F32))
    mine = jnp.concatenate(
        [
            jnp.concatenate(proj, axis=1),
            jnp.concatenate(sense, axis=1),
            jnp.concatenate(parts, axis=1),
        ],
        axis=0,
    )
    out[...] = mine
    big_out[0:block] = mine
    for ref, copy in zip((w_in, w_pair, spin_bias, rates), copies):
        copy[...] = ref[...]


def ripple(x, width):
    step = width
    while step < LANES:
        x = x + pltpu.roll(x, step, 1)
        step *= 2
    return x


def spread(x, w, width):
    return ripple(jnp.where(iota(x.shape, 1) // width == w, x, 0.0), width)


def wide(x):
    return jnp.concatenate([x, x], axis=1)


def thirds(x):
    high = x.astype(BF16)
    rest = x - high.astype(F32)
    middle = rest.astype(BF16)
    return high, middle, (rest - middle.astype(F32)).astype(BF16)


def features(packed, rows, feats):
    parts = [packed] + [pltpu.roll(packed, LANES - feats * k, 1) for k in range(1, rows // 8)]
    return jnp.concatenate(parts, axis=0)


def prepare_kernel(walkers, rows, own, w_pair, spin_bias, rates, basis_out, rows_out, *mix_out):
    width = w_pair.shape[0]
    lanes = PACK * width
    spin_at = 6 * walkers
    feats = spin_at + 8
    if mix_out:
        sel = flag(iota((LANES, width), 0) % width == iota((LANES, width), 1)).astype(BF16)
        sel_t = flag(iota((width, LANES), 1) % width == iota((width, LANES), 0)).astype(BF16)
        same = iota((LANES, LANES), 0) // width == iota((LANES, LANES), 1) // width
        high, low = [
            jnp.where(same, dot(dot(sel, part).astype(BF16), sel_t), 0.0) for part in split(w_pair[...])
        ]
        top = jnp.concatenate([high, low], axis=1)
        bottom = jnp.concatenate([high, jnp.zeros_like(high)], axis=1)
        mix_out[0][...] = jnp.concatenate([top, bottom], axis=0).astype(BF16)
    sel_wide = flag(iota((width, lanes), 1) % width == iota((width, lanes), 0))
    rate_row = dot_exact(rates[...], sel_wide) * (0.5 / (jnp.pi * jnp.pi))
    bias_rows = dot_exact(spin_bias[...], sel_wide)
    bias_low, bias_step = bias_rows[0:1], bias_rows[1:2] - bias_rows[0:1]
    proj, sense = own[0:rows], own[rows : 2 * rows]
    feat = features(own[2 * rows : 2 * rows + 8], rows, feats)[:, :feats]
    feat_row = iota((feats, lanes), 0)
    tile = 0
    columns = [(wide(spread(proj, w, width)), wide(spread(sense, w, width))) for w in range(walkers)]
    groups, parts, spins = [], [], []
    for h in range(rows // PACK):
        group = flag(iota((rows, lanes), 1) // width + PACK * h == iota((rows, lanes), 0))
        cols = dot_exact(feat, group, ((0,), (0,)))
        spins.append(cols[spin_at : spin_at + 1])
        groups.append(group)
        parts.append(thirds(jnp.where(feat_row == spin_at + 1, -3.0, cols) * rate_row))
    for w in range(walkers):
        keep = ((feat_row < spin_at) & (feat_row % walkers == w)) | (feat_row == spin_at + 1)
        for h in range(rows // PACK):
            high, middle, low = [jnp.where(keep, p.astype(F32), 0.0).astype(BF16) for p in parts[h]]
            basis_out[:, tile * lanes : (tile + 1) * lanes] = jnp.concatenate(
                [high, middle, low, high, middle, high], axis=0
            )
            row_proj = jnp.sum(columns[w][0] * groups[h], axis=0, keepdims=True)
            row_sense = jnp.sum(columns[w][1] * groups[h], axis=0, keepdims=True)
            rows_out[8 * tile : 8 * tile + 8] = jnp.concatenate(
                [
                    row_sense,
                    row_proj + bias_low + (1.0 - spins[h]) * bias_step,
                    (2.0 * spins[h] - 1.0) * bias_step,
                    spins[h],
                    jnp.zeros((4, lanes), F32),
                ],
                axis=0,
            )
            tile += 1


def fold(x):
    return jnp.sum(x.reshape(x.shape[0] // 8, 8, x.shape[1]), axis=0)


def pair_kernel(walkers, width, rows, total, sets, *refs):
    side, gathered = refs[0], refs[1]
    bigs = refs[2 : 2 + sets]
    bases = refs[2 + sets : 2 + 2 * sets]
    row_sets = refs[2 + 2 * sets : 2 + 3 * sets]
    mix = refs[2 + 3 * sets]
    sens_out, keep_out, send_out, lhs, rhs = refs[3 + 3 * sets :]
    spin_at = 6 * walkers
    feats = spin_at + 8
    lanes = PACK * width
    per_walker = rows // PACK
    tiles = walkers * per_walker
    block = 2 * rows + 8
    starts = [block * s for s in range(gathered.shape[0] // block)]
    proj = jnp.concatenate([gathered[s : s + rows] for s in starts], axis=0)
    sense = jnp.concatenate([gathered[s + rows : s + 2 * rows] for s in starts], axis=0)
    feat = jnp.concatenate(
        [features(gathered[s + 2 * rows : s + block], rows, feats) for s in starts], axis=0
    )
    count = feat.shape[0]
    spin = jnp.broadcast_to(feat[:, spin_at : spin_at + 1], (count, LANES))
    feat = jnp.where(iota(feat.shape, 1) < feats, feat, 0.0)
    high, middle, low = [p.astype(F32) for p in thirds(feat)]
    first = high + pltpu.roll(high, feats, 1) + pltpu.roll(high, 2 * feats, 1)
    first = first + pltpu.roll(middle, 3 * feats, 1)
    second = middle + pltpu.roll(low, feats, 1)
    left = jnp.concatenate([first, second[:, : 2 * feats]], axis=1).astype(BF16)
    halves = [slice(0, LANES), slice(LANES, lanes)]
    group = 2 * count * per_walker
    sums = [[None] * tiles for _ in range(sets)]
    for w in range(walkers):
        col_proj, col_sense = spread(proj, w, width), spread(sense, w, width)
        for n in range(sets):
            base = (w * sets + n) * group
            for k in range(per_walker):
                tile = w * per_walker + k
                radial = jnp.exp(dot(left, bases[n][:, tile * lanes : (tile + 1) * lanes]))
                for i, half in enumerate(halves):
                    at = base + (2 * k + i) * count
                    high, low = split(radial[:, half])
                    lhs[at : at + count] = jnp.concatenate([high, low], axis=1)
            mixed = dot(lhs[base : base + group], mix[...])
            mixed = mixed[:, :LANES] + mixed[:, LANES:]
            for k in range(per_walker):
                tile = w * per_walker + k
                acc = []
                for i, half in enumerate(halves):
                    at = (2 * k + i) * count
                    row_sense = row_sets[n][8 * tile : 8 * tile + 1, half]
                    row_base = row_sets[n][8 * tile + 1 : 8 * tile + 2, half]
                    row_turn = row_sets[n][8 * tile + 2 : 8 * tile + 3, half]
                    z = mixed[at : at + count] + col_proj + (row_base + spin * row_turn)
                    if n == 0:
                        lane = iota((rows, LANES), 1) // width + PACK * k + i * (LANES // width)
                        far = jnp.where(lane == iota((rows, LANES), 0), 16384.0, 0.0)
                        z = jnp.concatenate([z[:rows] + far, z[rows:]], axis=0)
                    m = jnp.tanh(z)
                    slope = 1.0 - m * m
                    high, low = split(slope * row_sense)
                    rhs[base + at : base + at + count] = jnp.concatenate([high, low], axis=1)
                    acc.append((fold(slope), fold(slope * spin), fold(slope * col_sense), fold(m)))
                sums[n][tile] = [jnp.concatenate([a, b], axis=1) for a, b in zip(*acc)]
    tn = ((0,), (0,))
    grams = dot(lhs[...], rhs[...], tn)
    lane8 = iota((8, lanes), 1) // width == iota((8, lanes), 0)
    lane = iota((8, LANES), 1) // width
    sens, mean = [], []
    same_row = jnp.zeros((1, lanes), F32)
    all_row = jnp.zeros((1, lanes), F32)

    def column(row):
        row = jnp.where(lane8, jnp.broadcast_to(row, (8, lanes)), 0.0)
        return ripple(row[:, :LANES] + row[:, LANES:], width)

    for n in range(sets):
        for t in range(tiles):
            slope, turn, col, act = [jnp.sum(x, axis=0, keepdims=True) for x in sums[n][t]]
            row_sense = row_sets[n][8 * t : 8 * t + 1]
            row_spin = row_sets[n][8 * t + 3 : 8 * t + 4]
            own = row_sense * slope
            sens.append(column(own + col))
            mean.append(column(act - 1.0 if n == 0 else act))
            all_row = all_row + own
            same_row = same_row + (1.0 - row_spin) * own
            same_row = same_row + (2.0 * row_spin - 1.0) * (row_sense * turn)
    sens = jnp.concatenate(sens, axis=0)
    mean = jnp.concatenate(mean, axis=0)
    n_rows = walkers * rows
    sens_out[...] = sens[:n_rows]
    lane_all = iota(sens.shape, 1) // width
    both = jnp.where(lane_all == 0, sens, jnp.where(lane_all == 1, mean, 0.0))
    high, low = split(both)
    chunks = (bigs[0].shape[0] - block) // n_rows
    inputs = [
        jnp.concatenate(
            [b[block + k * n_rows : block + (k + 1) * n_rows] for k in range(chunks)], axis=1
        )
        for b in bigs
    ]
    inputs = jnp.concatenate(inputs, axis=0).astype(BF16)
    weights = dot(high, inputs, tn) + dot(low, inputs, tn)
    hidden_width = inputs.shape[1] // 2
    in_part = weights[:width, :hidden_width]
    out_part = weights[width : 2 * width, hidden_width:] / total
    quad = grams[:LANES, :LANES] + grams[LANES:, :LANES] + (grams[:LANES, LANES:] + grams[LANES:, LANES:])
    pair = quad[0:width]
    for k in range(1, LANES // width):
        pair = pair + pltpu.roll(quad[k * width : (k + 1) * width], LANES - k * width, 1)
    tail = jnp.where(lane == 0, pair[0:8], 0.0)
    for k in range(1, width // 8):
        tail = tail + jnp.where(lane == k, pltpu.roll(pair[8 * k : 8 * k + 8], k * width, 1), 0.0)
    pick = iota((8, lanes), 0)
    bias = jnp.where(
        pick == 0,
        jnp.broadcast_to(all_row - same_row, (8, lanes)),
        jnp.where(pick == 1, jnp.broadcast_to(same_row, (8, lanes)), 0.0),
    )
    bias = ripple(bias[:, :LANES] + bias[:, LANES:], width)
    half = hidden_width // 2
    low_half = jnp.concatenate([in_part[:, :half], out_part[:, :half], tail], axis=0)
    high_half = jnp.concatenate([in_part[:, half:], out_part[:, half:], bias], axis=0)
    first = side[0] == 0
    flat = low_half.shape[0]
    keep_out[0:flat] = jnp.where(first, low_half, high_half)
    send_out[0:flat] = jnp.where(first, high_half, low_half)
    place = iota((rows, LANES), 1) // width
    for n in range(1, sets):
        packed = jnp.zeros((rows, LANES), F32)
        for w in range(walkers):
            part = sens[n * n_rows + w * rows : n * n_rows + (w + 1) * rows]
            packed = packed + jnp.where(place == w, part, 0.0)
        at = flat + (n - 1) * rows
        keep_out[at : at + rows] = packed
        send_out[at : at + rows] = jnp.zeros((rows, LANES), F32)


def hidden_kernel(offsets, sens, w_in, *refs):
    received, grad_out = refs[:-1], refs[-1]
    walkers, rows, _ = grad_out.shape
    width = w_in.shape[0]
    total = []
    for w in range(walkers):
        part = sens[w * rows : (w + 1) * rows]
        for at, ref in zip(offsets, received):
            part = part + spread(ref[at : at + rows], w, width)
        total.append(part)
    high, low = split(jnp.concatenate(total, axis=0))
    both = jnp.concatenate([high[:, :width], low[:, :width]], axis=1)
    grad = dot(both, jnp.concatenate([w_in[...], w_in[...]], axis=0))
    for w in range(walkers):
        grad_out[w] = grad[w * rows : (w + 1) * rows].astype(BF16)


def finish_kernel(side, mine, other, w_in_grad, w_pair_grad, bias_grad, w_out_grad):
    width = w_pair_grad.shape[0]
    first = side[0] == 0
    low = jnp.where(first, mine[...], other[...])
    high = jnp.where(first, other[...], mine[...])
    full = jnp.concatenate([low, high], axis=1)
    w_in_grad[...] = full[:width]
    w_out_grad[...] = full[width : 2 * width]
    tail = full[2 * width :]
    for k in range(width // 8):
        w_pair_grad[8 * k : 8 * k + 8] = tail[:, k * width : (k + 1) * width]
    at = (width // 8) * width
    bias_grad[...] = tail[0:2, at : at + width]


VMEM = pl.BlockSpec(memory_space=pltpu.VMEM)
SMEM = pl.BlockSpec(memory_space=pltpu.SMEM)


def near(x):
    return pltpu.with_memory_space_constraint(x, pltpu.VMEM)


def swap(x, axis, size, mask):
    return lax.ppermute(x, axis, [(i, i ^ mask) for i in range(size)])


def stages(blocks):
    groups, top = [], blocks
    while top > 2:
        groups.append((top // 4, top // 2, 3 * top // 4))
        top //= 4
    if top == 2:
        groups.append((1,))
    return groups


def join(mine, got):
    mine = mine + got[0]
    return mine + (got[1] + got[2]) if len(got) == 3 else mine


def on_device(hidden, cotangent, positions, spins, w_in, w_pair, spin_bias, rates, w_out):
    blocks = lax.axis_size("elec")
    walkers, rows, hidden_width = hidden.shape
    width = w_in.shape[1]
    total = rows * blocks
    side = lax.axis_index("walk").astype(jnp.int32).reshape(1)
    block = 2 * rows + 8
    n_rows = walkers * rows
    lanes = PACK * width
    tiles = n_rows // PACK
    groups = stages(blocks)
    col_groups, row_masks = groups[:-1], groups[-1]
    sets = 1 + len(row_masks)
    payload, big, *params = pl.pallas_call(
        functools.partial(embed_kernel, total),
        out_shape=(
            pltpu.VMEM((block, LANES), F32),
            pltpu.VMEM((block + n_rows * 2 * hidden_width // LANES, LANES), F32),
            pltpu.VMEM((width, hidden_width), BF16),
            pltpu.VMEM((width, width), F32),
            pltpu.VMEM((2, width), F32),
            pltpu.VMEM((1, width), F32),
        ),
        in_specs=[VMEM] * 9,
        out_specs=(VMEM,) * 6,
        name="embed",
    )(
        hidden,
        cotangent,
        positions.transpose(1, 0, 2),
        spins.reshape(1, rows),
        w_in.T,
        w_out,
        w_pair,
        spin_bias,
        rates.reshape(1, width),
    )
    w_in_near, *params = [near(p) for p in params]
    bigs = [big] + [swap(big, "elec", blocks, m) for m in row_masks]
    gathered = [payload]
    for masks in col_groups:
        whole = gathered[0] if len(gathered) == 1 else jnp.concatenate(gathered, axis=0)
        gathered = [whole] + [swap(whole, "elec", blocks, m) for m in masks]
    columns = gathered[0] if len(gathered) == 1 else jnp.concatenate(gathered, axis=0)
    depth = 6 * (6 * walkers + 8)

    def prepare(source, first):
        extra = (pltpu.VMEM((lanes, lanes), BF16),) if first else ()
        return pl.pallas_call(
            functools.partial(prepare_kernel, walkers, rows),
            out_shape=(
                pltpu.VMEM((depth, tiles * lanes), BF16),
                pltpu.VMEM((8 * tiles, lanes), F32),
            )
            + extra,
            in_specs=[VMEM] * 4,
            out_specs=(VMEM,) * (2 + len(extra)),
            name="prepare_own" if first else "prepare_row",
        )(near(source), *params)

    basis, row_terms, mix = prepare(payload, True)
    bases, row_sets = [basis], [row_terms]
    for source in bigs[1:]:
        basis, row_terms = prepare(source, False)
        bases.append(basis)
        row_sets.append(row_terms)
    flat = 2 * width + 8
    tall = flat + (sets - 1) * rows
    depth = columns.shape[0] // block * rows * 2 * tiles * sets
    operands = [columns, *bigs, *bases, *row_sets, mix]
    sens, keep, send = pl.pallas_call(
        functools.partial(pair_kernel, walkers, width, rows, total, sets),
        out_shape=(
            pltpu.VMEM((n_rows, LANES), F32),
            pltpu.VMEM((tall, LANES), F32),
            pltpu.VMEM((tall, LANES), F32),
        ),
        in_specs=[SMEM] + [VMEM] * len(operands),
        out_specs=(VMEM,) * 3,
        scratch_shapes=[pltpu.VMEM((depth, 2 * LANES), BF16)] * 2,
        name="pairs",
    )(side, *[near(x) for x in operands])
    mine = keep + swap(send, "walk", 2, 1)
    got = [swap(mine, "elec", blocks, m) for m in row_masks]
    offsets = tuple(flat + n * rows for n in range(len(got)))
    grad = pl.pallas_call(
        functools.partial(hidden_kernel, offsets),
        out_shape=jax.ShapeDtypeStruct(hidden.shape, BF16),
        in_specs=[VMEM] * (2 + len(got)),
        out_specs=VMEM,
        name="hidden_grad",
    )(near(sens), w_in_near, *[near(g) for g in got])
    mine = join(mine[:flat], [g[:flat] for g in got])
    for masks in reversed(col_groups):
        got = [swap(mine, "elec", blocks, m) for m in masks]
        mine = join(mine, got)
    other = swap(mine, "walk", 2, 1)
    w_in_grad, w_pair_grad, spin_bias_grad, w_out_grad = pl.pallas_call(
        finish_kernel,
        out_shape=(
            jax.ShapeDtypeStruct((width, hidden_width), F32),
            jax.ShapeDtypeStruct((width, width), F32),
            jax.ShapeDtypeStruct((2, width), F32),
            jax.ShapeDtypeStruct((width, hidden_width), F32),
        ),
        in_specs=[SMEM, VMEM, VMEM],
        out_specs=(VMEM,) * 4,
        name="finish",
    )(side, near(mine), near(other))
    return (grad, w_in_grad.T, w_pair_grad, spin_bias_grad, w_out_grad)


def solution(mesh):
    return jax.shard_map(
        on_device,
        mesh=mesh,
        in_specs=(
            P(("groups", "walk"), "elec", None),
            P(("groups", "walk"), "elec", None),
            P(("groups", "walk"), None, "elec"),
            P(("groups", "elec")),
            P(),
            P(),
            P(),
            P(),
            P(),
        ),
        out_specs=(
            P(("groups", "walk"), "elec", None),
            P("groups", None),
            P("groups", None),
            P("groups", None),
            P("groups", None),
        ),
        check_vma=False,
    )
```

profile of v0, /device:TPU:0, one launch (start us, length us, event | category | flops | bytes accessed | tf_op | source)
XLA Modules:
  0.0 29.6 jit_solution(13038428682176800512)
XLA Ops:
  0.6 1.1 %embed.1 = (f32[40,128]{1,0:T(8,128)S(1)}, f32[296,128]{1,0:T(8,128)S(1)}, bf16[32,256]{1,0:T(8,128)(2,1)S(1)}, f32[32,32]{1,0:T(8,128)S(1)}, f32[2,32]{1,0:T(2,128)S(1)}, /*index=5*/f32[1,32]{1,0:T(1,128)S(1)}) custom-call(bf16[4,16,256]{2,1,0:T(8,128)(2,1)} %hid.1, bf16[4,16,256]{2,1,0:T(8,128)(2,1)} %cot.1, f32[3,4,16]{2,1,0:T(4,128)} %bitcast.7, ...), custom_call_target="tpu_custom_call" | custom-call | tf_op jit(solution)/shard_map/embed/pallas_call | solution.py:368
  1.7 3.1 %collective-permute-start.3 = (f32[296,128]{1,0:T(8,128)S(1)}, f32[296,128]{1,0:T(8,128)S(1)}, u32[]{:S(2)}, u32[]{:S(2)}) collective-permute-start(f32[296,128]{1,0:T(8,128)S(1)} %get-tuple-element.24.refs_2_), channel_id=1, source_target_pairs={{0,2},{2,0},{4,6},{6,4},{8,10},{10,8},{12,14},{14,12},{1,3},{3,1},... | collective-permute-start | bytes 454664 | tf_op jit(solution)/shard_map/ppermute | solution.py:337
  4.8 3.6 %collective-permute-start.2 = (f32[40,128]{1,0:T(8,128)S(1)}, f32[40,128]{1,0:T(8,128)S(1)}, u32[]{:S(2)}, u32[]{:S(2)}) collective-permute-start(f32[40,128]{1,0:T(8,128)S(1)} %get-tuple-element.23.own), channel_id=1, source_target_pairs={{0,12},{2,14},{4,8},{6,10},{8,4},{10,6},{12,0},{14,2},{1,13},{3,15... | collective-permute-start | bytes 61448 | tf_op jit(solution)/shard_map/ppermute | solution.py:337
  8.4 0.0 collective-permute-start.1
  8.4 0.8 %collective-permute-start = (f32[40,128]{1,0:T(8,128)S(1)}, f32[40,128]{1,0:T(8,128)S(1)}, u32[]{:S(2)}, u32[]{:S(2)}) collective-permute-start(f32[40,128]{1,0:T(8,128)S(1)} %get-tuple-element.23.own), channel_id=1, source_target_pairs={{0,4},{2,6},{4,0},{6,2},{8,12},{10,14},{12,8},{14,10},{1,5},{3,7},... | collective-permute-start | bytes 61448 | tf_op jit(solution)/shard_map/ppermute | solution.py:337
  9.2 0.4 %prepare_own.1 = (bf16[192,2048]{1,0:T(8,128)(2,1)S(1)}, f32[64,256]{1,0:T(8,128)S(1)}, bf16[256,256]{1,0:T(8,128)(2,1)S(1)}) custom-call(f32[40,128]{1,0:T(8,128)S(1)} %get-tuple-element.23.own, f32[32,32]{1,0:T(8,128)S(1)} %get-tuple-element.25.w_pair, f32[2,32]{1,0:T(2,128)S(1)} %get-tuple-element.26.spin_bias, f32[1,32]{1,0:T(1,128)S(1)} %get-tuple-element.27.rates), custom_call_target="tpu_custom_call" | custom-call | tf_op jit(solution)/shard_map/prepare_own/pallas_call | solution.py:403
  9.6 1.0 %collective-permute-done.2 = f32[40,128]{1,0:T(8,128)S(1)} collective-permute-done((f32[40,128]{1,0:T(8,128)S(1)}, f32[40,128]{1,0:T(8,128)S(1)}, u32[]{:S(2)}, u32[]{:S(2)}) %collective-permute-start.2) | collective-permute-done | bytes 20512 | tf_op jit(solution)/shard_map/ppermute | solution.py:337
  10.6 2.5 %collective-permute-done.1 = f32[40,128]{1,0:T(8,128)S(1)} collective-permute-done((f32[40,128]{1,0:T(8,128)S(1)}, f32[40,128]{1,0:T(8,128)S(1)}, u32[]{:S(2)}, u32[]{:S(2)}) %collective-permute-start.1) | collective-permute-done | bytes 20512 | tf_op jit(solution)/shard_map/ppermute | solution.py:337
  13.1 0.0 collective-permute-done
  13.1 0.0 collective-permute-done.3.own.refs_3_
  13.1 0.4 %prepare_row.1 = (bf16[192,2048]{1,0:T(8,128)(2,1)S(1)}, f32[64,256]{1,0:T(8,128)S(1)}) custom-call(f32[296,128]{1,0:T(8,128)S(1)} %collective-permute-done.3.own.refs_3_, f32[32,32]{1,0:T(8,128)S(1)} %get-tuple-element.25.w_pair, f32[2,32]{1,0:T(2,128)S(1)} %get-tuple-element.26.spin_bias, f32[1,32]{1,0:T(1,128)S(1)} %get-tuple-element.27.rates), custom_call_target="tpu_custom_call" | custom-call | tf_op jit(solution)/shard_map/prepare_row/pallas_call | solution.py:403
  13.5 2.1 %pairs.1 = (f32[64,128]{1,0:T(8,128)S(1)}, f32[88,128]{1,0:T(8,128)S(1)}, f32[88,128]{1,0:T(8,128)S(1)}) custom-call(s32[1]{0:T(128)} %bitcast.refs_0_.side, f32[160,128]{1,0:T(8,128)S(1)} %pad_maximum_fusion.refs_1_, f32[296,128]{1,0:T(8,128)S(1)} %get-tuple-element.24.refs_2_, f32[296,128]{1,0:T(8,128)S(1)} %collective-permute-done.3.own.refs_3_, ...), custom_call_target="tpu_custom_call" | custom-call | tf_op jit(solution)/shard_map/pairs/pallas_call | solution.py:425
  15.5 0.0 collective-permute-start.4
  15.6 1.2 %collective-permute-done.4 = f32[88,128]{1,0:T(8,128)S(1)} collective-permute-done((f32[88,128]{1,0:T(8,128)S(1)}, f32[88,128]{1,0:T(8,128)S(1)}, u32[]{:S(2)}, u32[]{:S(2)}) %collective-permute-start.4) | collective-permute-done | bytes 45088 | tf_op jit(solution)/shard_map/ppermute | solution.py:337
  16.8 0.6 %collective-permute-start.5 = (f32[88,128]{1,0:T(8,128)S(1)}, f32[88,128]{1,0:T(8,128)S(1)}, u32[]{:S(2)}, u32[]{:S(2)}) collective-permute-start(f32[88,128]{1,0:T(8,128)S(1)} %add.15), channel_id=1, source_target_pairs={{0,2},{2,0},{4,6},{6,4},{8,10},{10,8},{12,14},{14,12},{1,3},{3,1},... | collective-permute-start | bytes 135176 | tf_op jit(solution)/shard_map/ppermute | solution.py:337
  17.4 3.5 %collective-permute-done.5.refs_0_ = f32[88,128]{1,0:T(8,128)S(1)} collective-permute-done((f32[88,128]{1,0:T(8,128)S(1)}, f32[88,128]{1,0:T(8,128)S(1)}, u32[]{:S(2)}, u32[]{:S(2)}) %collective-permute-start.5) | collective-permute-done | bytes 45088 | tf_op jit(solution)/shard_map/ppermute | solution.py:337
  20.9 1.4 %collective-permute-start.8 = (f32[72,128]{1,0:T(8,128)S(1)}, f32[72,128]{1,0:T(8,128)S(1)}, u32[]{:S(2)}, u32[]{:S(2)}) collective-permute-start(f32[72,128]{1,0:T(8,128)S(1)} %slice_add_fusion), channel_id=1, source_target_pairs={{0,12},{2,14},{4,8},{6,10},{8,4},{10,6},{12,0},{14,2},{1,13},{3,15... | collective-permute-start | bytes 110600 | tf_op jit(solution)/shard_map/ppermute | solution.py:337
  22.4 0.6 %collective-permute-start.7 = (f32[72,128]{1,0:T(8,128)S(1)}, f32[72,128]{1,0:T(8,128)S(1)}, u32[]{:S(2)}, u32[]{:S(2)}) collective-permute-start(f32[72,128]{1,0:T(8,128)S(1)} %slice_add_fusion), channel_id=1, source_target_pairs={{0,8},{2,10},{4,12},{6,14},{8,0},{10,2},{12,4},{14,6},{1,9},{3,11}... | collective-permute-start | bytes 110600 | tf_op jit(solution)/shard_map/ppermute | solution.py:337
  23.0 2.3 %collective-permute-start.6 = (f32[72,128]{1,0:T(8,128)S(1)}, f32[72,128]{1,0:T(8,128)S(1)}, u32[]{:S(2)}, u32[]{:S(2)}) collective-permute-start(f32[72,128]{1,0:T(8,128)S(1)} %slice_add_fusion), channel_id=1, source_target_pairs={{0,4},{2,6},{4,0},{6,2},{8,12},{10,14},{12,8},{14,10},{1,5},{3,7},... | collective-permute-start | bytes 110600 | tf_op jit(solution)/shard_map/ppermute | solution.py:337
  25.3 1.4 %collective-permute-done.8 = f32[72,128]{1,0:T(8,128)S(1)} collective-permute-done((f32[72,128]{1,0:T(8,128)S(1)}, f32[72,128]{1,0:T(8,128)S(1)}, u32[]{:S(2)}, u32[]{:S(2)}) %collective-permute-start.8) | collective-permute-done | bytes 36896 | tf_op jit(solution)/shard_map/ppermute | solution.py:337
  26.7 0.6 %collective-permute-done.7 = f32[72,128]{1,0:T(8,128)S(1)} collective-permute-done((f32[72,128]{1,0:T(8,128)S(1)}, f32[72,128]{1,0:T(8,128)S(1)}, u32[]{:S(2)}, u32[]{:S(2)}) %collective-permute-start.7) | collective-permute-done | bytes 36896 | tf_op jit(solution)/shard_map/ppermute | solution.py:337
  27.2 0.4 %collective-permute-done.6 = f32[72,128]{1,0:T(8,128)S(1)} collective-permute-done((f32[72,128]{1,0:T(8,128)S(1)}, f32[72,128]{1,0:T(8,128)S(1)}, u32[]{:S(2)}, u32[]{:S(2)}) %collective-permute-start.6) | collective-permute-done | bytes 36896 | tf_op jit(solution)/shard_map/ppermute | solution.py:337
  27.6 0.1 collective-permute-start.9
  27.7 1.0 %hidden_grad.1 = bf16[4,16,256]{2,1,0:T(8,128)(2,1)} custom-call(f32[64,128]{1,0:T(8,128)S(1)} %get-tuple-element.33.sens, bf16[32,256]{1,0:T(8,128)(2,1)S(1)} %get-tuple-element.34.w_in, f32[88,128]{1,0:T(8,128)S(1)} %collective-permute-done.5.refs_0_), custom_call_target="tpu_custom_call" | custom-call | tf_op jit(solution)/shard_map/hidden_grad/pallas_call | solution.py:440
  28.7 0.2 collective-permute-done.9.other
  28.9 0.7 %finish.1 = (f32[32,256]{1,0:T(8,128)}, f32[32,32]{1,0:T(8,128)}, f32[2,32]{1,0:T(2,128)}, f32[32,256]{1,0:T(8,128)}) custom-call(s32[1]{0:T(128)} %bitcast.refs_0_.side, f32[72,128]{1,0:T(8,128)S(1)} %add_add_fusion.mine, f32[72,128]{1,0:T(8,128)S(1)} %collective-permute-done.9.other), custom_call_target="tpu_custom_call" | custom-call | tf_op jit(solution)/shard_map/finish/pallas_call | solution.py:452
  (4 shorter events, 0.0 us)
Async XLA Ops:
  1.7 11.4 %collective-permute-start.3 = (f32[296,128]{1,0:T(8,128)S(1)}, f32[296,128]{1,0:T(8,128)S(1)}, u32[]{:S(2)}, u32[]{:S(2)}) collective-permute-start(f32[296,128]{1,0:T(8,128)S(1)} %get-tuple-element.24.refs_2_), channel_id=1, source_target_pairs={{0,2},{2,0},{4,6},{6,4},{8,10},{10,8},{12,14},{14,12},{1,3},{3,1},... | collective-permute-start | bytes 454664 | tf_op jit(solution)/shard_map/ppermute | solution.py:337
  4.8 5.8 %collective-permute-start.2 = (f32[40,128]{1,0:T(8,128)S(1)}, f32[40,128]{1,0:T(8,128)S(1)}, u32[]{:S(2)}, u32[]{:S(2)}) collective-permute-start(f32[40,128]{1,0:T(8,128)S(1)} %get-tuple-element.23.own), channel_id=1, source_target_pairs={{0,12},{2,14},{4,8},{6,10},{8,4},{10,6},{12,0},{14,2},{1,13},{3,15... | collective-permute-start | bytes 61448 | tf_op jit(solution)/shard_map/ppermute | solution.py:337
  8.4 4.7 %collective-permute-start.1 = (f32[40,128]{1,0:T(8,128)S(1)}, f32[40,128]{1,0:T(8,128)S(1)}, u32[]{:S(2)}, u32[]{:S(2)}) collective-permute-start(f32[40,128]{1,0:T(8,128)S(1)} %get-tuple-element.23.own), channel_id=1, source_target_pairs={{0,8},{2,10},{4,12},{6,14},{8,0},{10,2},{12,4},{14,6},{1,9},{3,11}... | collective-permute-start | bytes 61448 | tf_op jit(solution)/shard_map/ppermute | solution.py:337
  8.4 4.7 %collective-permute-start = (f32[40,128]{1,0:T(8,128)S(1)}, f32[40,128]{1,0:T(8,128)S(1)}, u32[]{:S(2)}, u32[]{:S(2)}) collective-permute-start(f32[40,128]{1,0:T(8,128)S(1)} %get-tuple-element.23.own), channel_id=1, source_target_pairs={{0,4},{2,6},{4,0},{6,2},{8,12},{10,14},{12,8},{14,10},{1,5},{3,7},... | collective-permute-start | bytes 61448 | tf_op jit(solution)/shard_map/ppermute | solution.py:337
  15.5 1.2 %collective-permute-start.4 = (f32[88,128]{1,0:T(8,128)S(1)}, f32[88,128]{1,0:T(8,128)S(1)}, u32[]{:S(2)}, u32[]{:S(2)}) collective-permute-start(f32[88,128]{1,0:T(8,128)S(1)} %get-tuple-element.36), channel_id=1, source_target_pairs={{0,1},{1,0},{2,3},{3,2},{4,5},{5,4},{6,7},{7,6},{8,9},{9,8},{10,11... | collective-permute-start | bytes 135176 | tf_op jit(solution)/shard_map/ppermute | solution.py:337
  16.8 4.1 %collective-permute-start.5 = (f32[88,128]{1,0:T(8,128)S(1)}, f32[88,128]{1,0:T(8,128)S(1)}, u32[]{:S(2)}, u32[]{:S(2)}) collective-permute-start(f32[88,128]{1,0:T(8,128)S(1)} %add.15), channel_id=1, source_target_pairs={{0,2},{2,0},{4,6},{6,4},{8,10},{10,8},{12,14},{14,12},{1,3},{3,1},... | collective-permute-start | bytes 135176 | tf_op jit(solution)/shard_map/ppermute | solution.py:337
  20.9 5.8 %collective-permute-start.8 = (f32[72,128]{1,0:T(8,128)S(1)}, f32[72,128]{1,0:T(8,128)S(1)}, u32[]{:S(2)}, u32[]{:S(2)}) collective-permute-start(f32[72,128]{1,0:T(8,128)S(1)} %slice_add_fusion), channel_id=1, source_target_pairs={{0,12},{2,14},{4,8},{6,10},{8,4},{10,6},{12,0},{14,2},{1,13},{3,15... | collective-permute-start | bytes 110600 | tf_op jit(solution)/shard_map/ppermute | solution.py:337
  22.4 4.9 %collective-permute-start.7 = (f32[72,128]{1,0:T(8,128)S(1)}, f32[72,128]{1,0:T(8,128)S(1)}, u32[]{:S(2)}, u32[]{:S(2)}) collective-permute-start(f32[72,128]{1,0:T(8,128)S(1)} %slice_add_fusion), channel_id=1, source_target_pairs={{0,8},{2,10},{4,12},{6,14},{8,0},{10,2},{12,4},{14,6},{1,9},{3,11}... | collective-permute-start | bytes 110600 | tf_op jit(solution)/shard_map/ppermute | solution.py:337
  23.0 4.6 %collective-permute-start.6 = (f32[72,128]{1,0:T(8,128)S(1)}, f32[72,128]{1,0:T(8,128)S(1)}, u32[]{:S(2)}, u32[]{:S(2)}) collective-permute-start(f32[72,128]{1,0:T(8,128)S(1)} %slice_add_fusion), channel_id=1, source_target_pairs={{0,4},{2,6},{4,0},{6,2},{8,12},{10,14},{12,8},{14,10},{1,5},{3,7},... | collective-permute-start | bytes 110600 | tf_op jit(solution)/shard_map/ppermute | solution.py:337
  27.6 1.3 %collective-permute-start.9 = (f32[72,128]{1,0:T(8,128)S(1)}, f32[72,128]{1,0:T(8,128)S(1)}, u32[]{:S(2)}, u32[]{:S(2)}) collective-permute-start(f32[72,128]{1,0:T(8,128)S(1)} %add_add_fusion.mine), channel_id=1, source_target_pairs={{0,1},{1,0},{2,3},{3,2},{4,5},{5,4},{6,7},{7,6},{8,9},{9,8},{10,11... | collective-permute-start | bytes 110600 | tf_op jit(solution)/shard_map/ppermute | solution.py:337
where the time goes:
time: 29.8 us; the launch traced here: 29.6 us
  starting transfers between devices  12.5 us (42%)
  waiting for transfers between devices  10.8 us (36%)
  Pallas kernels  5.57 us (19%)
  between operations  0.7 us (2%)
    ppermute x10, starting transfers between devices, swap(): return lax.ppermute(x, axis, [(i, i ^ mask) for i in range(size)])  12.5 us
    ppermute x10, waiting for transfers between devices, swap(): return lax.ppermute(x, axis, [(i, i ^ mask) for i in range(size)])  10.8 us
    pallas_call x1, Pallas kernels, on_device(): pl.pallas_call(functools.partial(pair_kernel, walkers, width, rows, total...  2.06 us
    pallas_call x1, Pallas kernels, on_device(): pl.pallas_call(functools.partial(embed_kernel, total), out_shape=(pltpu.V...  1.07 us
    pallas_call x1, Pallas kernels, on_device(): pl.pallas_call(functools.partial(hidden_kernel, offsets), out_shape=jax.S...  0.96 us
    pallas_call x2, Pallas kernels, prepare(): pl.pallas_call(functools.partial(prepare_kernel, walkers, rows), out_shap...  0.81 us
    pallas_call x1, Pallas kernels, on_device(): pl.pallas_call(finish_kernel, out_shape=(jax.ShapeDtypeStruct((width, hid...  0.68 us
  transfers between devices with their start and end apart: 10, of which 8 were waited for; matrix products, arithmetic and copies ran while one was open for 0% of the time, Pallas kernels for 5%

commit v1 on v0

--- a/solution.py
+++ b/solution.py
@@ -1,4 +1,5 @@
 import functools
+import math
 
 import jax
 import jax.numpy as jnp
@@ -116,7 +117,7 @@
         bottom = jnp.concatenate([high, jnp.zeros_like(high)], axis=1)
         mix_out[0][...] = jnp.concatenate([top, bottom], axis=0).astype(BF16)
     sel_wide = flag(iota((width, lanes), 1) % width == iota((width, lanes), 0))
-    rate_row = dot_exact(rates[...], sel_wide) * (0.5 / (jnp.pi * jnp.pi))
+    rate_row = dot_exact(rates[...], sel_wide) * (0.5 / (math.pi**2 * math.log(2.0)))
     bias_rows = dot_exact(spin_bias[...], sel_wide)
     bias_low, bias_step = bias_rows[0:1], bias_rows[1:2] - bias_rows[0:1]
     proj, sense = own[0:rows], own[rows : 2 * rows]
@@ -144,7 +145,7 @@
                 [
                     row_sense,
                     row_proj + bias_low + (1.0 - spins[h]) * bias_step,
-                    (2.0 * spins[h] - 1.0) * bias_step,
+                    row_proj + bias_low + spins[h] * bias_step,
                     spins[h],
                     jnp.zeros((4, lanes), F32),
                 ],
@@ -177,7 +178,7 @@
         [features(gathered[s + 2 * rows : s + block], rows, feats) for s in starts], axis=0
     )
     count = feat.shape[0]
-    spin = jnp.broadcast_to(feat[:, spin_at : spin_at + 1], (count, LANES))
+    is_up = jnp.broadcast_to(feat[:, spin_at : spin_at + 1], (count, LANES)) > 0.5
     feat = jnp.where(iota(feat.shape, 1) < feats, feat, 0.0)
     high, middle, low = [p.astype(F32) for p in thirds(feat)]
     first = high + pltpu.roll(high, feats, 1) + pltpu.roll(high, 2 * feats, 1)
@@ -193,7 +194,7 @@
             base = (w * sets + n) * group
             for k in range(per_walker):
                 tile = w * per_walker + k
-                radial = jnp.exp(dot(left, bases[n][:, tile * lanes : (tile + 1) * lanes]))
+                radial = jnp.exp2(dot(left, bases[n][:, tile * lanes : (tile + 1) * lanes]))
                 for i, half in enumerate(halves):
                     at = base + (2 * k + i) * count
                     high, low = split(radial[:, half])
@@ -208,16 +209,16 @@
                     row_sense = row_sets[n][8 * tile : 8 * tile + 1, half]
                     row_base = row_sets[n][8 * tile + 1 : 8 * tile + 2, half]
                     row_turn = row_sets[n][8 * tile + 2 : 8 * tile + 3, half]
-                    z = mixed[at : at + count] + col_proj + (row_base + spin * row_turn)
+                    z = mixed[at : at + count] + col_proj + jnp.where(is_up, row_turn, row_base)
                     if n == 0:
-                        lane = iota((rows, LANES), 1) // width + PACK * k + i * (LANES // width)
-                        far = jnp.where(lane == iota((rows, LANES), 0), 16384.0, 0.0)
+                        owner = iota((rows, LANES), 1) // width + PACK * k + i * (LANES // width)
+                        far = jnp.where(owner == iota((rows, LANES), 0), 16384.0, 0.0)
                         z = jnp.concatenate([z[:rows] + far, z[rows:]], axis=0)
                     m = jnp.tanh(z)
                     slope = 1.0 - m * m
                     high, low = split(slope * row_sense)
                     rhs[base + at : base + at + count] = jnp.concatenate([high, low], axis=1)
-                    acc.append((fold(slope), fold(slope * spin), fold(slope * col_sense), fold(m)))
+                    acc.append((fold(slope), fold(jnp.where(is_up, slope, 0.0)), fold(slope * col_sense), fold(m)))
                 sums[n][tile] = [jnp.concatenate([a, b], axis=1) for a, b in zip(*acc)]
     tn = ((0,), (0,))
     grams = dot(lhs[...], rhs[...], tn)
@@ -281,7 +282,7 @@
     first = side[0] == 0
     flat = low_half.shape[0]
     keep_out[0:flat] = jnp.where(first, low_half, high_half)
-    send_out[0:flat] = jnp.where(first, high_half, low_half)
+    send_out[...] = jnp.where(first, high_half, low_half)
     place = iota((rows, LANES), 1) // width
     for n in range(1, sets):
         packed = jnp.zeros((rows, LANES), F32)
@@ -290,7 +291,6 @@
             packed = packed + jnp.where(place == w, part, 0.0)
         at = flat + (n - 1) * rows
         keep_out[at : at + rows] = packed
-        send_out[at : at + rows] = jnp.zeros((rows, LANES), F32)
 
 
 def hidden_kernel(offsets, sens, w_in, *refs):
@@ -427,15 +427,16 @@
         out_shape=(
             pltpu.VMEM((n_rows, LANES), F32),
             pltpu.VMEM((tall, LANES), F32),
-            pltpu.VMEM((tall, LANES), F32),
+            pltpu.VMEM((flat, LANES), F32),
         ),
         in_specs=[SMEM] + [VMEM] * len(operands),
         out_specs=(VMEM,) * 3,
         scratch_shapes=[pltpu.VMEM((depth, 2 * LANES), BF16)] * 2,
         name="pairs",
     )(side, *[near(x) for x in operands])
-    mine = keep + swap(send, "walk", 2, 1)
-    got = [swap(mine, "elec", blocks, m) for m in row_masks]
+    near_part = swap(send, "walk", 2, 1)
+    got = [swap(keep, "elec", blocks, m) for m in row_masks]
+    cross = [swap(send, ("elec", "walk"), 2 * blocks, 2 * m + 1) for m in row_masks]
     offsets = tuple(flat + n * rows for n in range(len(got)))
     grad = pl.pallas_call(
         functools.partial(hidden_kernel, offsets),
@@ -444,7 +445,7 @@
         out_specs=VMEM,
         name="hidden_grad",
     )(near(sens), w_in_near, *[near(g) for g in got])
-    mine = join(mine[:flat], [g[:flat] for g in got])
+    mine = join(keep[:flat] + near_part, [g[:flat] + c for g, c in zip(got, cross)])
     for masks in reversed(col_groups):
         got = [swap(mine, "elec", blocks, m) for m in masks]
         mine = join(mine, got)

time: 29.8 us -> 29.1 us (0.977)
  waiting for transfers between devices: 10.8 us -> 8.55 us
  starting transfers between devices: 12.5 us -> 14.1 us
    ppermute x10 -> x11, waiting for transfers between devices: 10.8 us -> 8.55 us  [swap(): return lax.ppermute(x, axis, [(i, i ^ mask) for i in range(size)])]
    ppermute x10 -> x11, starting transfers between devices: 12.5 us -> 14.1 us  [swap(): return lax.ppermute(x, axis, [(i, i ^ mask) for i in range(size)])]
  transfers between devices with their start and end apart: 10 -> 11, of which waited for: 8 -> 7; matrix products, arithmetic and copies ran while one was open for 0% -> 0% of each run, Pallas kernels for 5% -> 5%
where the time goes in v1:
time: 29.1 us; the launch traced here: 29 us
  starting transfers between devices  14.1 us (48%)
  waiting for transfers between devices  8.55 us (29%)
  Pallas kernels  5.55 us (19%)
  between operations  0.7 us (2%)
    ppermute x11, starting transfers between devices, swap(): return lax.ppermute(x, axis, [(i, i ^ mask) for i in range(size)])  14.1 us
    ppermute x11, waiting for transfers between devices, swap(): return lax.ppermute(x, axis, [(i, i ^ mask) for i in range(size)])  8.55 us
    pallas_call x1, Pallas kernels, on_device(): pl.pallas_call(functools.partial(pair_kernel, walkers, width, rows, total...  2.04 us
    pallas_call x1, Pallas kernels, on_device(): pl.pallas_call(functools.partial(embed_kernel, total), out_shape=(pltpu.V...  1.07 us
    pallas_call x1, Pallas kernels, on_device(): pl.pallas_call(functools.partial(hidden_kernel, offsets), out_shape=jax.S...  0.96 us
    pallas_call x2, Pallas kernels, prepare(): pl.pallas_call(functools.partial(prepare_kernel, walkers, rows), out_shap...  0.81 us
    pallas_call x1, Pallas kernels, on_device(): pl.pallas_call(finish_kernel, out_shape=(jax.ShapeDtypeStruct((width, hid...  0.68 us
  transfers between devices with their start and end apart: 11, of which 7 were waited for; matrix products, arithmetic and copies ran while one was open for 0% of the time, Pallas kernels for 5%

profile of v1, /device:TPU:0, one launch (start us, length us, event | category | flops | bytes accessed | tf_op | source)
XLA Modules:
  0.0 29.0 jit_solution(1659767950764838169)
XLA Ops:
  0.6 1.1 %embed.1 = (f32[40,128]{1,0:T(8,128)S(1)}, f32[296,128]{1,0:T(8,128)S(1)}, bf16[32,256]{1,0:T(8,128)(2,1)S(1)}, f32[32,32]{1,0:T(8,128)S(1)}, f32[2,32]{1,0:T(2,128)S(1)}, /*index=5*/f32[1,32]{1,0:T(1,128)S(1)}) custom-call(bf16[4,16,256]{2,1,0:T(8,128)(2,1)} %hid.1, bf16[4,16,256]{2,1,0:T(8,128)(2,1)} %cot.1, f32[3,4,16]{2,1,0:T(4,128)} %bitcast.7, ...), custom_call_target="tpu_custom_call" | custom-call | tf_op jit(solution)/shard_map/embed/pallas_call | solution.py:368
  1.7 3.1 %collective-permute-start.3 = (f32[296,128]{1,0:T(8,128)S(1)}, f32[296,128]{1,0:T(8,128)S(1)}, u32[]{:S(2)}, u32[]{:S(2)}) collective-permute-start(f32[296,128]{1,0:T(8,128)S(1)} %get-tuple-element.24.refs_2_), channel_id=1, source_target_pairs={{0,2},{2,0},{4,6},{6,4},{8,10},{10,8},{12,14},{14,12},{1,3},{3,1},... | collective-permute-start | bytes 454664 | tf_op jit(solution)/shard_map/ppermute | solution.py:337
  4.8 3.6 %collective-permute-start.2 = (f32[40,128]{1,0:T(8,128)S(1)}, f32[40,128]{1,0:T(8,128)S(1)}, u32[]{:S(2)}, u32[]{:S(2)}) collective-permute-start(f32[40,128]{1,0:T(8,128)S(1)} %get-tuple-element.23.own), channel_id=1, source_target_pairs={{0,12},{2,14},{4,8},{6,10},{8,4},{10,6},{12,0},{14,2},{1,13},{3,15... | collective-permute-start | bytes 61448 | tf_op jit(solution)/shard_map/ppermute | solution.py:337
  8.4 0.0 collective-permute-start.1
  8.4 0.8 %collective-permute-start = (f32[40,128]{1,0:T(8,128)S(1)}, f32[40,128]{1,0:T(8,128)S(1)}, u32[]{:S(2)}, u32[]{:S(2)}) collective-permute-start(f32[40,128]{1,0:T(8,128)S(1)} %get-tuple-element.23.own), channel_id=1, source_target_pairs={{0,4},{2,6},{4,0},{6,2},{8,12},{10,14},{12,8},{14,10},{1,5},{3,7},... | collective-permute-start | bytes 61448 | tf_op jit(solution)/shard_map/ppermute | solution.py:337
  9.2 0.4 %prepare_own.1 = (bf16[192,2048]{1,0:T(8,128)(2,1)S(1)}, f32[64,256]{1,0:T(8,128)S(1)}, bf16[256,256]{1,0:T(8,128)(2,1)S(1)}) custom-call(f32[40,128]{1,0:T(8,128)S(1)} %get-tuple-element.23.own, f32[32,32]{1,0:T(8,128)S(1)} %get-tuple-element.25.w_pair, f32[2,32]{1,0:T(2,128)S(1)} %get-tuple-element.26.spin_bias, f32[1,32]{1,0:T(1,128)S(1)} %get-tuple-element.27.rates), custom_call_target="tpu_custom_call" | custom-call | tf_op jit(solution)/shard_map/prepare_own/pallas_call | solution.py:403
  9.6 1.0 %collective-permute-done.2 = f32[40,128]{1,0:T(8,128)S(1)} collective-permute-done((f32[40,128]{1,0:T(8,128)S(1)}, f32[40,128]{1,0:T(8,128)S(1)}, u32[]{:S(2)}, u32[]{:S(2)}) %collective-permute-start.2) | collective-permute-done | bytes 20512 | tf_op jit(solution)/shard_map/ppermute | solution.py:337
  10.6 2.5 %collective-permute-done.1 = f32[40,128]{1,0:T(8,128)S(1)} collective-permute-done((f32[40,128]{1,0:T(8,128)S(1)}, f32[40,128]{1,0:T(8,128)S(1)}, u32[]{:S(2)}, u32[]{:S(2)}) %collective-permute-start.1) | collective-permute-done | bytes 20512 | tf_op jit(solution)/shard_map/ppermute | solution.py:337
  13.1 0.0 collective-permute-done
  13.1 0.0 collective-permute-done.3.own.refs_3_
  13.1 0.4 %prepare_row.1 = (bf16[192,2048]{1,0:T(8,128)(2,1)S(1)}, f32[64,256]{1,0:T(8,128)S(1)}) custom-call(f32[296,128]{1,0:T(8,128)S(1)} %collective-permute-done.3.own.refs_3_, f32[32,32]{1,0:T(8,128)S(1)} %get-tuple-element.25.w_pair, f32[2,32]{1,0:T(2,128)S(1)} %get-tuple-element.26.spin_bias, f32[1,32]{1,0:T(1,128)S(1)} %get-tuple-element.27.rates), custom_call_target="tpu_custom_call" | custom-call | tf_op jit(solution)/shard_map/prepare_row/pallas_call | solution.py:403
  13.5 2.0 %pairs.1 = (f32[64,128]{1,0:T(8,128)S(1)}, f32[88,128]{1,0:T(8,128)S(1)}, f32[72,128]{1,0:T(8,128)S(1)}) custom-call(s32[1]{0:T(128)} %bitcast.refs_0_.side, f32[160,128]{1,0:T(8,128)S(1)} %pad_maximum_fusion.refs_1_, f32[296,128]{1,0:T(8,128)S(1)} %get-tuple-element.24.refs_2_, f32[296,128]{1,0:T(8,128)S(1)} %collective-permute-done.3.own.refs_3_, ...), custom_call_target="tpu_custom_call" | custom-call | tf_op jit(solution)/shard_map/pairs/pallas_call | solution.py:425
  15.5 0.5 %collective-permute-start.4 = (f32[88,128]{1,0:T(8,128)S(1)}, f32[88,128]{1,0:T(8,128)S(1)}, u32[]{:S(2)}, u32[]{:S(2)}) collective-permute-start(f32[88,128]{1,0:T(8,128)S(1)} %get-tuple-element.35), channel_id=1, source_target_pairs={{0,2},{2,0},{4,6},{6,4},{8,10},{10,8},{12,14},{14,12},{1,3},{3,1},... | collective-permute-start | bytes 135176 | tf_op jit(solution)/shard_map/ppermute | solution.py:337
  16.0 0.0 collective-permute-start.6
  16.0 1.6 %collective-permute-start.5 = (f32[72,128]{1,0:T(8,128)S(1)}, f32[72,128]{1,0:T(8,128)S(1)}, u32[]{:S(2)}, u32[]{:S(2)}) collective-permute-start(f32[72,128]{1,0:T(8,128)S(1)} %get-tuple-element.36), channel_id=1, source_target_pairs={{0,1},{1,0},{2,3},{3,2},{4,5},{5,4},{6,7},{7,6},{8,9},{9,8},{10,11... | collective-permute-start | bytes 110600 | tf_op jit(solution)/shard_map/ppermute | solution.py:337
  17.7 2.1 %collective-permute-done.6 = f32[72,128]{1,0:T(8,128)S(1)} collective-permute-done((f32[72,128]{1,0:T(8,128)S(1)}, f32[72,128]{1,0:T(8,128)S(1)}, u32[]{:S(2)}, u32[]{:S(2)}) %collective-permute-start.6) | collective-permute-done | bytes 36896 | tf_op jit(solution)/shard_map/ppermute | solution.py:337
  19.8 0.0 collective-permute-done.5
  19.8 0.2 collective-permute-done.4.refs_0_
  19.9 1.5 %collective-permute-start.9 = (f32[72,128]{1,0:T(8,128)S(1)}, f32[72,128]{1,0:T(8,128)S(1)}, u32[]{:S(2)}, u32[]{:S(2)}) collective-permute-start(f32[72,128]{1,0:T(8,128)S(1)} %fusion), channel_id=1, source_target_pairs={{0,12},{2,14},{4,8},{6,10},{8,4},{10,6},{12,0},{14,2},{1,13},{3,15... | collective-permute-start | bytes 110600 | tf_op jit(solution)/shard_map/ppermute | solution.py:337
  21.4 0.6 %collective-permute-start.8 = (f32[72,128]{1,0:T(8,128)S(1)}, f32[72,128]{1,0:T(8,128)S(1)}, u32[]{:S(2)}, u32[]{:S(2)}) collective-permute-start(f32[72,128]{1,0:T(8,128)S(1)} %fusion), channel_id=1, source_target_pairs={{0,8},{2,10},{4,12},{6,14},{8,0},{10,2},{12,4},{14,6},{1,9},{3,11}... | collective-permute-start | bytes 110600 | tf_op jit(solution)/shard_map/ppermute | solution.py:337
  22.1 2.3 %collective-permute-start.7 = (f32[72,128]{1,0:T(8,128)S(1)}, f32[72,128]{1,0:T(8,128)S(1)}, u32[]{:S(2)}, u32[]{:S(2)}) collective-permute-start(f32[72,128]{1,0:T(8,128)S(1)} %fusion), channel_id=1, source_target_pairs={{0,4},{2,6},{4,0},{6,2},{8,12},{10,14},{12,8},{14,10},{1,5},{3,7},... | collective-permute-start | bytes 110600 | tf_op jit(solution)/shard_map/ppermute | solution.py:337
  24.4 1.7 %collective-permute-done.9 = f32[72,128]{1,0:T(8,128)S(1)} collective-permute-done((f32[72,128]{1,0:T(8,128)S(1)}, f32[72,128]{1,0:T(8,128)S(1)}, u32[]{:S(2)}, u32[]{:S(2)}) %collective-permute-start.9) | collective-permute-done | bytes 36896 | tf_op jit(solution)/shard_map/ppermute | solution.py:337
  26.1 0.9 %collective-permute-done.8 = f32[72,128]{1,0:T(8,128)S(1)} collective-permute-done((f32[72,128]{1,0:T(8,128)S(1)}, f32[72,128]{1,0:T(8,128)S(1)}, u32[]{:S(2)}, u32[]{:S(2)}) %collective-permute-start.8) | collective-permute-done | bytes 36896 | tf_op jit(solution)/shard_map/ppermute | solution.py:337
  27.0 0.0 collective-permute-done.7
  27.0 0.1 collective-permute-start.10
  27.1 1.0 %hidden_grad.1 = bf16[4,16,256]{2,1,0:T(8,128)(2,1)} custom-call(f32[64,128]{1,0:T(8,128)S(1)} %get-tuple-element.33.sens, bf16[32,256]{1,0:T(8,128)(2,1)S(1)} %get-tuple-element.34.w_in, f32[88,128]{1,0:T(8,128)S(1)} %collective-permute-done.4.refs_0_), custom_call_target="tpu_custom_call" | custom-call | tf_op jit(solution)/shard_map/hidden_grad/pallas_call | solution.py:441
  28.0 0.2 collective-permute-done.10.other
  28.3 0.7 %finish.1 = (f32[32,256]{1,0:T(8,128)}, f32[32,32]{1,0:T(8,128)}, f32[2,32]{1,0:T(2,128)}, f32[32,256]{1,0:T(8,128)}) custom-call(s32[1]{0:T(128)} %bitcast.refs_0_.side, f32[72,128]{1,0:T(8,128)S(1)} %add_add_fusion.mine, f32[72,128]{1,0:T(8,128)S(1)} %collective-permute-done.10.other), custom_call_target="tpu_custom_call" | custom-call | tf_op jit(solution)/shard_map/finish/pallas_call | solution.py:453
  (3 shorter events, 0.0 us)
Async XLA Ops:
  1.7 11.4 %collective-permute-start.3 = (f32[296,128]{1,0:T(8,128)S(1)}, f32[296,128]{1,0:T(8,128)S(1)}, u32[]{:S(2)}, u32[]{:S(2)}) collective-permute-start(f32[296,128]{1,0:T(8,128)S(1)} %get-tuple-element.24.refs_2_), channel_id=1, source_target_pairs={{0,2},{2,0},{4,6},{6,4},{8,10},{10,8},{12,14},{14,12},{1,3},{3,1},... | collective-permute-start | bytes 454664 | tf_op jit(solution)/shard_map/ppermute | solution.py:337
  4.8 5.8 %collective-permute-start.2 = (f32[40,128]{1,0:T(8,128)S(1)}, f32[40,128]{1,0:T(8,128)S(1)}, u32[]{:S(2)}, u32[]{:S(2)}) collective-permute-start(f32[40,128]{1,0:T(8,128)S(1)} %get-tuple-element.23.own), channel_id=1, source_target_pairs={{0,12},{2,14},{4,8},{6,10},{8,4},{10,6},{12,0},{14,2},{1,13},{3,15... | collective-permute-start | bytes 61448 | tf_op jit(solution)/shard_map/ppermute | solution.py:337
  8.4 4.7 %collective-permute-start.1 = (f32[40,128]{1,0:T(8,128)S(1)}, f32[40,128]{1,0:T(8,128)S(1)}, u32[]{:S(2)}, u32[]{:S(2)}) collective-permute-start(f32[40,128]{1,0:T(8,128)S(1)} %get-tuple-element.23.own), channel_id=1, source_target_pairs={{0,8},{2,10},{4,12},{6,14},{8,0},{10,2},{12,4},{14,6},{1,9},{3,11}... | collective-permute-start | bytes 61448 | tf_op jit(solution)/shard_map/ppermute | solution.py:337
  8.4 4.7 %collective-permute-start = (f32[40,128]{1,0:T(8,128)S(1)}, f32[40,128]{1,0:T(8,128)S(1)}, u32[]{:S(2)}, u32[]{:S(2)}) collective-permute-start(f32[40,128]{1,0:T(8,128)S(1)} %get-tuple-element.23.own), channel_id=1, source_target_pairs={{0,4},{2,6},{4,0},{6,2},{8,12},{10,14},{12,8},{14,10},{1,5},{3,7},... | collective-permute-start | bytes 61448 | tf_op jit(solution)/shard_map/ppermute | solution.py:337
  15.5 4.4 %collective-permute-start.4 = (f32[88,128]{1,0:T(8,128)S(1)}, f32[88,128]{1,0:T(8,128)S(1)}, u32[]{:S(2)}, u32[]{:S(2)}) collective-permute-start(f32[88,128]{1,0:T(8,128)S(1)} %get-tuple-element.35), channel_id=1, source_target_pairs={{0,2},{2,0},{4,6},{6,4},{8,10},{10,8},{12,14},{14,12},{1,3},{3,1},... | collective-permute-start | bytes 135176 | tf_op jit(solution)/shard_map/ppermute | solution.py:337
  16.0 3.7 %collective-permute-start.6 = (f32[72,128]{1,0:T(8,128)S(1)}, f32[72,128]{1,0:T(8,128)S(1)}, u32[]{:S(2)}, u32[]{:S(2)}) collective-permute-start(f32[72,128]{1,0:T(8,128)S(1)} %get-tuple-element.36), channel_id=1, source_target_pairs={{0,3},{1,2},{2,1},{3,0},{4,7},{5,6},{6,5},{7,4},{8,11},{9,10},{10,... | collective-permute-start | bytes 110600 | tf_op jit(solution)/shard_map/ppermute | solution.py:337
  16.0 3.7 %collective-permute-start.5 = (f32[72,128]{1,0:T(8,128)S(1)}, f32[72,128]{1,0:T(8,128)S(1)}, u32[]{:S(2)}, u32[]{:S(2)}) collective-permute-start(f32[72,128]{1,0:T(8,128)S(1)} %get-tuple-element.36), channel_id=1, source_target_pairs={{0,1},{1,0},{2,3},{3,2},{4,5},{5,4},{6,7},{7,6},{8,9},{9,8},{10,11... | collective-permute-start | bytes 110600 | tf_op jit(solution)/shard_map/ppermute | solution.py:337
  19.9 6.1 %collective-permute-start.9 = (f32[72,128]{1,0:T(8,128)S(1)}, f32[72,128]{1,0:T(8,128)S(1)}, u32[]{:S(2)}, u32[]{:S(2)}) collective-permute-start(f32[72,128]{1,0:T(8,128)S(1)} %fusion), channel_id=1, source_target_pairs={{0,12},{2,14},{4,8},{6,10},{8,4},{10,6},{12,0},{14,2},{1,13},{3,15... | collective-permute-start | bytes 110600 | tf_op jit(solution)/shard_map/ppermute | solution.py:337
  21.4 5.5 %collective-permute-start.8 = (f32[72,128]{1,0:T(8,128)S(1)}, f32[72,128]{1,0:T(8,128)S(1)}, u32[]{:S(2)}, u32[]{:S(2)}) collective-permute-start(f32[72,128]{1,0:T(8,128)S(1)} %fusion), channel_id=1, source_target_pairs={{0,8},{2,10},{4,12},{6,14},{8,0},{10,2},{12,4},{14,6},{1,9},{3,11}... | collective-permute-start | bytes 110600 | tf_op jit(solution)/shard_map/ppermute | solution.py:337
  22.1 4.9 %collective-permute-start.7 = (f32[72,128]{1,0:T(8,128)S(1)}, f32[72,128]{1,0:T(8,128)S(1)}, u32[]{:S(2)}, u32[]{:S(2)}) collective-permute-start(f32[72,128]{1,0:T(8,128)S(1)} %fusion), channel_id=1, source_target_pairs={{0,4},{2,6},{4,0},{6,2},{8,12},{10,14},{12,8},{14,10},{1,5},{3,7},... | collective-permute-start | bytes 110600 | tf_op jit(solution)/shard_map/ppermute | solution.py:337
  27.0 1.3 %collective-permute-start.10 = (f32[72,128]{1,0:T(8,128)S(1)}, f32[72,128]{1,0:T(8,128)S(1)}, u32[]{:S(2)}, u32[]{:S(2)}) collective-permute-start(f32[72,128]{1,0:T(8,128)S(1)} %add_add_fusion.mine), channel_id=1, source_target_pairs={{0,1},{1,0},{2,3},{3,2},{4,5},{5,4},{6,7},{7,6},{8,9},{9,8},{10,11... | collective-permute-start | bytes 110600 | tf_op jit(solution)/shard_map/ppermute | solution.py:337

commit v2 on v1

--- a/solution.py
+++ b/solution.py
@@ -338,13 +338,15 @@
 
 
 def stages(blocks):
-    groups, top = [], blocks
-    while top > 2:
-        groups.append((top // 4, top // 2, 3 * top // 4))
-        top //= 4
-    if top == 2:
-        groups.append((1,))
-    return groups
+    row = min(2, blocks // 2)
+    bits = [1 << k for k in range(blocks.bit_length() - 1) if 1 << k != row]
+    groups = []
+    while len(bits) > 1:
+        high, low = bits.pop(), bits.pop()
+        groups.append((low, high, low ^ high))
+    if bits:
+        groups.append((bits.pop(),))
+    return groups + [(row,)]
 
 
 def join(mine, got):
@@ -357,13 +359,18 @@
     walkers, rows, hidden_width = hidden.shape
     width = w_in.shape[1]
     total = rows * blocks
-    side = lax.axis_index("walk").astype(jnp.int32).reshape(1)
     block = 2 * rows + 8
     n_rows = walkers * rows
     lanes = PACK * width
     tiles = n_rows // PACK
     groups = stages(blocks)
     col_groups, row_masks = groups[:-1], groups[-1]
+    turns = sum(masks[1] for masks in col_groups if len(masks) == 3)
+    side = lax.axis_index("walk").astype(jnp.int32)
+    for bit in range(blocks.bit_length()):
+        if turns >> bit & 1:
+            side = side ^ (lax.axis_index("elec").astype(jnp.int32) >> bit & 1)
+    side = side.reshape(1)
     sets = 1 + len(row_masks)
     payload, big, *params = pl.pallas_call(
         functools.partial(embed_kernel, total),
@@ -447,7 +454,10 @@
     )(near(sens), w_in_near, *[near(g) for g in got])
     mine = join(keep[:flat] + near_part, [g[:flat] + c for g, c in zip(got, cross)])
     for masks in reversed(col_groups):
-        got = [swap(mine, "elec", blocks, m) for m in masks]
+        got = [
+            swap(mine, ("elec", "walk"), 2 * blocks, 2 * m + (m & turns).bit_count() % 2)
+            for m in masks
+        ]
         mine = join(mine, got)
     other = swap(mine, "walk", 2, 1)
     w_in_grad, w_pair_grad, spin_bias_grad, w_out_grad = pl.pallas_call(

time: 29.1 us -> 28.7 us (0.986)
  no operation moved by 1% of the time
where the time goes in v2:
time: 28.7 us; the launch traced here: 28.6 us
  starting transfers between devices  14 us (49%)
  waiting for transfers between devices  8.32 us (29%)
  Pallas kernels  5.55 us (19%)
  between operations  0.69 us (2%)
    ppermute x11, starting transfers between devices, swap(): return lax.ppermute(x, axis, [(i, i ^ mask) for i in range(size)])  14 us
    ppermute x11, waiting for transfers between devices, swap(): return lax.ppermute(x, axis, [(i, i ^ mask) for i in range(size)])  8.32 us
    pallas_call x1, Pallas kernels, on_device(): pl.pallas_call(functools.partial(pair_kernel, walkers, width, rows, total...  2.03 us
    pallas_call x1, Pallas kernels, on_device(): pl.pallas_call(functools.partial(embed_kernel, total), out_shape=(pltpu.V...  1.07 us
    pallas_call x1, Pallas kernels, on_device(): pl.pallas_call(functools.partial(hidden_kernel, offsets), out_shape=jax.S...  0.96 us
    pallas_call x2, Pallas kernels, prepare(): pl.pallas_call(functools.partial(prepare_kernel, walkers, rows), out_shap...  0.81 us
    pallas_call x1, Pallas kernels, on_device(): pl.pallas_call(finish_kernel, out_shape=(jax.ShapeDtypeStruct((width, hid...  0.68 us
  transfers between devices with their start and end apart: 11, of which 7 were waited for; matrix products, arithmetic and copies ran while one was open for 0% of the time, Pallas kernels for 5%

profile of v2, /device:TPU:0, one launch (start us, length us, event | category | flops | bytes accessed | tf_op | source)
XLA Modules:
  0.0 28.6 jit_solution(11508438214671776285)
XLA Ops:
  0.6 1.1 %embed.1 = (f32[40,128]{1,0:T(8,128)S(1)}, f32[296,128]{1,0:T(8,128)S(1)}, bf16[32,256]{1,0:T(8,128)(2,1)S(1)}, f32[32,32]{1,0:T(8,128)S(1)}, f32[2,32]{1,0:T(2,128)S(1)}, /*index=5*/f32[1,32]{1,0:T(1,128)S(1)}) custom-call(bf16[4,16,256]{2,1,0:T(8,128)(2,1)} %hid.1, bf16[4,16,256]{2,1,0:T(8,128)(2,1)} %cot.1, f32[3,4,16]{2,1,0:T(4,128)} %bitcast.7, ...), custom_call_target="tpu_custom_call" | custom-call | tf_op jit(solution)/shard_map/embed/pallas_call | solution.py:375
  1.7 3.1 %collective-permute-start.3 = (f32[296,128]{1,0:T(8,128)S(1)}, f32[296,128]{1,0:T(8,128)S(1)}, u32[]{:S(2)}, u32[]{:S(2)}) collective-permute-start(f32[296,128]{1,0:T(8,128)S(1)} %get-tuple-element.24.refs_2_), channel_id=1, source_target_pairs={{0,4},{2,6},{4,0},{6,2},{8,12},{10,14},{12,8},{14,10},{1,5},{3,7},... | collective-permute-start | bytes 454664 | tf_op jit(solution)/shard_map/ppermute | solution.py:337
  4.8 3.5 %collective-permute-start.2 = (f32[40,128]{1,0:T(8,128)S(1)}, f32[40,128]{1,0:T(8,128)S(1)}, u32[]{:S(2)}, u32[]{:S(2)}) collective-permute-start(f32[40,128]{1,0:T(8,128)S(1)} %get-tuple-element.23.own), channel_id=1, source_target_pairs={{0,10},{2,8},{4,14},{6,12},{8,2},{10,0},{12,6},{14,4},{1,11},{3,9}... | collective-permute-start | bytes 61448 | tf_op jit(solution)/shard_map/ppermute | solution.py:337
  8.4 0.3 %collective-permute-start.1 = (f32[40,128]{1,0:T(8,128)S(1)}, f32[40,128]{1,0:T(8,128)S(1)}, u32[]{:S(2)}, u32[]{:S(2)}) collective-permute-start(f32[40,128]{1,0:T(8,128)S(1)} %get-tuple-element.23.own), channel_id=1, source_target_pairs={{0,8},{2,10},{4,12},{6,14},{8,0},{10,2},{12,4},{14,6},{1,9},{3,11}... | collective-permute-start | bytes 61448 | tf_op jit(solution)/shard_map/ppermute | solution.py:337
  8.7 0.5 %collective-permute-start = (f32[40,128]{1,0:T(8,128)S(1)}, f32[40,128]{1,0:T(8,128)S(1)}, u32[]{:S(2)}, u32[]{:S(2)}) collective-permute-start(f32[40,128]{1,0:T(8,128)S(1)} %get-tuple-element.23.own), channel_id=1, source_target_pairs={{0,2},{2,0},{4,6},{6,4},{8,10},{10,8},{12,14},{14,12},{1,3},{3,1},... | collective-permute-start | bytes 61448 | tf_op jit(solution)/shard_map/ppermute | solution.py:337
  9.2 0.4 %prepare_own.1 = (bf16[192,2048]{1,0:T(8,128)(2,1)S(1)}, f32[64,256]{1,0:T(8,128)S(1)}, bf16[256,256]{1,0:T(8,128)(2,1)S(1)}) custom-call(f32[40,128]{1,0:T(8,128)S(1)} %get-tuple-element.23.own, f32[32,32]{1,0:T(8,128)S(1)} %get-tuple-element.25.w_pair, f32[2,32]{1,0:T(2,128)S(1)} %get-tuple-element.26.spin_bias, f32[1,32]{1,0:T(1,128)S(1)} %get-tuple-element.27.rates), custom_call_target="tpu_custom_call" | custom-call | tf_op jit(solution)/shard_map/prepare_own/pallas_call | solution.py:410
  9.6 0.8 %collective-permute-done.2 = f32[40,128]{1,0:T(8,128)S(1)} collective-permute-done((f32[40,128]{1,0:T(8,128)S(1)}, f32[40,128]{1,0:T(8,128)S(1)}, u32[]{:S(2)}, u32[]{:S(2)}) %collective-permute-start.2) | collective-permute-done | bytes 20512 | tf_op jit(solution)/shard_map/ppermute | solution.py:337
  10.4 2.7 %collective-permute-done.1 = f32[40,128]{1,0:T(8,128)S(1)} collective-permute-done((f32[40,128]{1,0:T(8,128)S(1)}, f32[40,128]{1,0:T(8,128)S(1)}, u32[]{:S(2)}, u32[]{:S(2)}) %collective-permute-start.1) | collective-permute-done | bytes 20512 | tf_op jit(solution)/shard_map/ppermute | solution.py:337
  13.2 0.0 collective-permute-done
  13.2 0.0 collective-permute-done.3.own.refs_3_
  13.2 0.4 %prepare_row.1 = (bf16[192,2048]{1,0:T(8,128)(2,1)S(1)}, f32[64,256]{1,0:T(8,128)S(1)}) custom-call(f32[296,128]{1,0:T(8,128)S(1)} %collective-permute-done.3.own.refs_3_, f32[32,32]{1,0:T(8,128)S(1)} %get-tuple-element.25.w_pair, f32[2,32]{1,0:T(2,128)S(1)} %get-tuple-element.26.spin_bias, f32[1,32]{1,0:T(1,128)S(1)} %get-tuple-element.27.rates), custom_call_target="tpu_custom_call" | custom-call | tf_op jit(solution)/shard_map/prepare_row/pallas_call | solution.py:410
  13.6 2.0 %pairs.1 = (f32[64,128]{1,0:T(8,128)S(1)}, f32[88,128]{1,0:T(8,128)S(1)}, f32[72,128]{1,0:T(8,128)S(1)}) custom-call(s32[1]{0:T(128)} %bitcast.refs_0_.side, f32[160,128]{1,0:T(8,128)S(1)} %pad_maximum_fusion.refs_1_, f32[296,128]{1,0:T(8,128)S(1)} %get-tuple-element.24.refs_2_, f32[296,128]{1,0:T(8,128)S(1)} %collective-permute-done.3.own.refs_3_, ...), custom_call_target="tpu_custom_call" | custom-call | tf_op jit(solution)/shard_map/pairs/pallas_call | solution.py:432
  15.6 0.4 %collective-permute-start.4 = (f32[88,128]{1,0:T(8,128)S(1)}, f32[88,128]{1,0:T(8,128)S(1)}, u32[]{:S(2)}, u32[]{:S(2)}) collective-permute-start(f32[88,128]{1,0:T(8,128)S(1)} %get-tuple-element.35), channel_id=1, source_target_pairs={{0,4},{2,6},{4,0},{6,2},{8,12},{10,14},{12,8},{14,10},{1,5},{3,7},... | collective-permute-start | bytes 135176 | tf_op jit(solution)/shard_map/ppermute | solution.py:337
  16.0 0.0 collective-permute-start.6
  16.0 1.8 %collective-permute-start.5 = (f32[72,128]{1,0:T(8,128)S(1)}, f32[72,128]{1,0:T(8,128)S(1)}, u32[]{:S(2)}, u32[]{:S(2)}) collective-permute-start(f32[72,128]{1,0:T(8,128)S(1)} %get-tuple-element.36), channel_id=1, source_target_pairs={{0,1},{1,0},{2,3},{3,2},{4,5},{5,4},{6,7},{7,6},{8,9},{9,8},{10,11... | collective-permute-start | bytes 110600 | tf_op jit(solution)/shard_map/ppermute | solution.py:337
  17.8 1.8 %collective-permute-done.6 = f32[72,128]{1,0:T(8,128)S(1)} collective-permute-done((f32[72,128]{1,0:T(8,128)S(1)}, f32[72,128]{1,0:T(8,128)S(1)}, u32[]{:S(2)}, u32[]{:S(2)}) %collective-permute-start.6) | collective-permute-done | bytes 36896 | tf_op jit(solution)/shard_map/ppermute | solution.py:337
  19.5 0.0 collective-permute-done.5
  19.5 0.3 %collective-permute-done.4.refs_0_ = f32[88,128]{1,0:T(8,128)S(1)} collective-permute-done((f32[88,128]{1,0:T(8,128)S(1)}, f32[88,128]{1,0:T(8,128)S(1)}, u32[]{:S(2)}, u32[]{:S(2)}) %collective-permute-start.4) | collective-permute-done | bytes 45088 | tf_op jit(solution)/shard_map/ppermute | solution.py:337
  19.9 1.8 %collective-permute-start.9 = (f32[72,128]{1,0:T(8,128)S(1)}, f32[72,128]{1,0:T(8,128)S(1)}, u32[]{:S(2)}, u32[]{:S(2)}) collective-permute-start(f32[72,128]{1,0:T(8,128)S(1)} %fusion), channel_id=1, source_target_pairs={{0,11},{1,10},{2,9},{3,8},{4,15},{5,14},{6,13},{7,12},{8,3},{9,2},... | collective-permute-start | bytes 110600 | tf_op jit(solution)/shard_map/ppermute | solution.py:337
  21.7 0.8 %collective-permute-start.8 = (f32[72,128]{1,0:T(8,128)S(1)}, f32[72,128]{1,0:T(8,128)S(1)}, u32[]{:S(2)}, u32[]{:S(2)}) collective-permute-start(f32[72,128]{1,0:T(8,128)S(1)} %fusion), channel_id=1, source_target_pairs={{0,9},{1,8},{2,11},{3,10},{4,13},{5,12},{6,15},{7,14},{8,1},{9,0},... | collective-permute-start | bytes 110600 | tf_op jit(solution)/shard_map/ppermute | solution.py:337
  22.5 1.5 %collective-permute-start.7 = (f32[72,128]{1,0:T(8,128)S(1)}, f32[72,128]{1,0:T(8,128)S(1)}, u32[]{:S(2)}, u32[]{:S(2)}) collective-permute-start(f32[72,128]{1,0:T(8,128)S(1)} %fusion), channel_id=1, source_target_pairs={{0,2},{1,3},{2,0},{3,1},{4,6},{5,7},{6,4},{7,5},{8,10},{9,11},{10,... | collective-permute-start | bytes 110600 | tf_op jit(solution)/shard_map/ppermute | solution.py:337
  24.0 2.1 %collective-permute-done.9 = f32[72,128]{1,0:T(8,128)S(1)} collective-permute-done((f32[72,128]{1,0:T(8,128)S(1)}, f32[72,128]{1,0:T(8,128)S(1)}, u32[]{:S(2)}, u32[]{:S(2)}) %collective-permute-start.9) | collective-permute-done | bytes 36896 | tf_op jit(solution)/shard_map/ppermute | solution.py:337
  26.2 0.0 collective-permute-done.8
  26.2 0.4 %collective-permute-done.7 = f32[72,128]{1,0:T(8,128)S(1)} collective-permute-done((f32[72,128]{1,0:T(8,128)S(1)}, f32[72,128]{1,0:T(8,128)S(1)}, u32[]{:S(2)}, u32[]{:S(2)}) %collective-permute-start.7) | collective-permute-done | bytes 36896 | tf_op jit(solution)/shard_map/ppermute | solution.py:337
  26.6 0.1 collective-permute-start.10
  26.7 1.0 %hidden_grad.1 = bf16[4,16,256]{2,1,0:T(8,128)(2,1)} custom-call(f32[64,128]{1,0:T(8,128)S(1)} %get-tuple-element.33.sens, bf16[32,256]{1,0:T(8,128)(2,1)S(1)} %get-tuple-element.34.w_in, f32[88,128]{1,0:T(8,128)S(1)} %collective-permute-done.4.refs_0_), custom_call_target="tpu_custom_call" | custom-call | tf_op jit(solution)/shard_map/hidden_grad/pallas_call | solution.py:448
  27.7 0.2 collective-permute-done.10.other
  27.9 0.7 %finish.1 = (f32[32,256]{1,0:T(8,128)}, f32[32,32]{1,0:T(8,128)}, f32[2,32]{1,0:T(2,128)}, f32[32,256]{1,0:T(8,128)}) custom-call(s32[1]{0:T(128)} %bitcast.refs_0_.side, f32[72,128]{1,0:T(8,128)S(1)} %add_add_fusion.mine, f32[72,128]{1,0:T(8,128)S(1)} %collective-permute-done.10.other), custom_call_target="tpu_custom_call" | custom-call | tf_op jit(solution)/shard_map/finish/pallas_call | solution.py:463
  (3 shorter events, 0.0 us)
Async XLA Ops:
  1.7 11.5 %collective-permute-start.3 = (f32[296,128]{1,0:T(8,128)S(1)}, f32[296,128]{1,0:T(8,128)S(1)}, u32[]{:S(2)}, u32[]{:S(2)}) collective-permute-start(f32[296,128]{1,0:T(8,128)S(1)} %get-tuple-element.24.refs_2_), channel_id=1, source_target_pairs={{0,4},{2,6},{4,0},{6,2},{8,12},{10,14},{12,8},{14,10},{1,5},{3,7},... | collective-permute-start | bytes 454664 | tf_op jit(solution)/shard_map/ppermute | solution.py:337
  4.8 5.6 %collective-permute-start.2 = (f32[40,128]{1,0:T(8,128)S(1)}, f32[40,128]{1,0:T(8,128)S(1)}, u32[]{:S(2)}, u32[]{:S(2)}) collective-permute-start(f32[40,128]{1,0:T(8,128)S(1)} %get-tuple-element.23.own), channel_id=1, source_target_pairs={{0,10},{2,8},{4,14},{6,12},{8,2},{10,0},{12,6},{14,4},{1,11},{3,9}... | collective-permute-start | bytes 61448 | tf_op jit(solution)/shard_map/ppermute | solution.py:337
  8.4 4.8 %collective-permute-start.1 = (f32[40,128]{1,0:T(8,128)S(1)}, f32[40,128]{1,0:T(8,128)S(1)}, u32[]{:S(2)}, u32[]{:S(2)}) collective-permute-start(f32[40,128]{1,0:T(8,128)S(1)} %get-tuple-element.23.own), channel_id=1, source_target_pairs={{0,8},{2,10},{4,12},{6,14},{8,0},{10,2},{12,4},{14,6},{1,9},{3,11}... | collective-permute-start | bytes 61448 | tf_op jit(solution)/shard_map/ppermute | solution.py:337
  8.7 4.5 %collective-permute-start = (f32[40,128]{1,0:T(8,128)S(1)}, f32[40,128]{1,0:T(8,128)S(1)}, u32[]{:S(2)}, u32[]{:S(2)}) collective-permute-start(f32[40,128]{1,0:T(8,128)S(1)} %get-tuple-element.23.own), channel_id=1, source_target_pairs={{0,2},{2,0},{4,6},{6,4},{8,10},{10,8},{12,14},{14,12},{1,3},{3,1},... | collective-permute-start | bytes 61448 | tf_op jit(solution)/shard_map/ppermute | solution.py:337
  15.6 4.2 %collective-permute-start.4 = (f32[88,128]{1,0:T(8,128)S(1)}, f32[88,128]{1,0:T(8,128)S(1)}, u32[]{:S(2)}, u32[]{:S(2)}) collective-permute-start(f32[88,128]{1,0:T(8,128)S(1)} %get-tuple-element.35), channel_id=1, source_target_pairs={{0,4},{2,6},{4,0},{6,2},{8,12},{10,14},{12,8},{14,10},{1,5},{3,7},... | collective-permute-start | bytes 135176 | tf_op jit(solution)/shard_map/ppermute | solution.py:337
  16.0 3.5 %collective-permute-start.6 = (f32[72,128]{1,0:T(8,128)S(1)}, f32[72,128]{1,0:T(8,128)S(1)}, u32[]{:S(2)}, u32[]{:S(2)}) collective-permute-start(f32[72,128]{1,0:T(8,128)S(1)} %get-tuple-element.36), channel_id=1, source_target_pairs={{0,5},{1,4},{2,7},{3,6},{4,1},{5,0},{6,3},{7,2},{8,13},{9,12},{10,... | collective-permute-start | bytes 110600 | tf_op jit(solution)/shard_map/ppermute | solution.py:337
  16.0 3.5 %collective-permute-start.5 = (f32[72,128]{1,0:T(8,128)S(1)}, f32[72,128]{1,0:T(8,128)S(1)}, u32[]{:S(2)}, u32[]{:S(2)}) collective-permute-start(f32[72,128]{1,0:T(8,128)S(1)} %get-tuple-element.36), channel_id=1, source_target_pairs={{0,1},{1,0},{2,3},{3,2},{4,5},{5,4},{6,7},{7,6},{8,9},{9,8},{10,11... | collective-permute-start | bytes 110600 | tf_op jit(solution)/shard_map/ppermute | solution.py:337
  19.9 6.3 %collective-permute-start.9 = (f32[72,128]{1,0:T(8,128)S(1)}, f32[72,128]{1,0:T(8,128)S(1)}, u32[]{:S(2)}, u32[]{:S(2)}) collective-permute-start(f32[72,128]{1,0:T(8,128)S(1)} %fusion), channel_id=1, source_target_pairs={{0,11},{1,10},{2,9},{3,8},{4,15},{5,14},{6,13},{7,12},{8,3},{9,2},... | collective-permute-start | bytes 110600 | tf_op jit(solution)/shard_map/ppermute | solution.py:337
  21.7 4.5 %collective-permute-start.8 = (f32[72,128]{1,0:T(8,128)S(1)}, f32[72,128]{1,0:T(8,128)S(1)}, u32[]{:S(2)}, u32[]{:S(2)}) collective-permute-start(f32[72,128]{1,0:T(8,128)S(1)} %fusion), channel_id=1, source_target_pairs={{0,9},{1,8},{2,11},{3,10},{4,13},{5,12},{6,15},{7,14},{8,1},{9,0},... | collective-permute-start | bytes 110600 | tf_op jit(solution)/shard_map/ppermute | solution.py:337
  22.5 4.1 %collective-permute-start.7 = (f32[72,128]{1,0:T(8,128)S(1)}, f32[72,128]{1,0:T(8,128)S(1)}, u32[]{:S(2)}, u32[]{:S(2)}) collective-permute-start(f32[72,128]{1,0:T(8,128)S(1)} %fusion), channel_id=1, source_target_pairs={{0,2},{1,3},{2,0},{3,1},{4,6},{5,7},{6,4},{7,5},{8,10},{9,11},{10,... | collective-permute-start | bytes 110600 | tf_op jit(solution)/shard_map/ppermute | solution.py:337
  26.6 1.3 %collective-permute-start.10 = (f32[72,128]{1,0:T(8,128)S(1)}, f32[72,128]{1,0:T(8,128)S(1)}, u32[]{:S(2)}, u32[]{:S(2)}) collective-permute-start(f32[72,128]{1,0:T(8,128)S(1)} %add_add_fusion.mine), channel_id=1, source_target_pairs={{0,1},{1,0},{2,3},{3,2},{4,5},{5,4},{6,7},{7,6},{8,9},{9,8},{10,11... | collective-permute-start | bytes 110600 | tf_op jit(solution)/shard_map/ppermute | solution.py:337

commit v3 on v2

--- a/solution.py
+++ b/solution.py
@@ -116,9 +116,13 @@
         top = jnp.concatenate([high, low], axis=1)
         bottom = jnp.concatenate([high, jnp.zeros_like(high)], axis=1)
         mix_out[0][...] = jnp.concatenate([top, bottom], axis=0).astype(BF16)
-    sel_wide = flag(iota((width, lanes), 1) % width == iota((width, lanes), 0))
-    rate_row = dot_exact(rates[...], sel_wide) * (0.5 / (math.pi**2 * math.log(2.0)))
-    bias_rows = dot_exact(spin_bias[...], sel_wide)
+    if mix_out:
+        sel_wide = flag(iota((width, lanes), 1) % width == iota((width, lanes), 0))
+        rate_row = dot_exact(rates[...], sel_wide) * (0.5 / (math.pi**2 * math.log(2.0)))
+        bias_rows = dot_exact(spin_bias[...], sel_wide)
+        mix_out[1][...] = jnp.concatenate([rate_row, bias_rows], axis=0)
+    else:
+        rate_row, bias_rows = rates[...], spin_bias[...]
     bias_low, bias_step = bias_rows[0:1], bias_rows[1:2] - bias_rows[0:1]
     proj, sense = own[0:rows], own[rows : 2 * rows]
     feat = features(own[2 * rows : 2 * rows + 8], rows, feats)[:, :feats]
@@ -152,6 +156,10 @@
                 axis=0,
             )
             tile += 1
+
+
+def prepare_row_kernel(walkers, rows, own, w_pair, terms, basis_out, rows_out):
+    prepare_kernel(walkers, rows, own, w_pair, terms.at[1:3], terms.at[0:1], basis_out, rows_out)
 
 
 def fold(x):
@@ -405,24 +413,23 @@
     columns = gathered[0] if len(gathered) == 1 else jnp.concatenate(gathered, axis=0)
     depth = 6 * (6 * walkers + 8)
 
-    def prepare(source, first):
-        extra = (pltpu.VMEM((lanes, lanes), BF16),) if first else ()
-        return pl.pallas_call(
-            functools.partial(prepare_kernel, walkers, rows),
-            out_shape=(
-                pltpu.VMEM((depth, tiles * lanes), BF16),
-                pltpu.VMEM((8 * tiles, lanes), F32),
-            )
-            + extra,
-            in_specs=[VMEM] * 4,
-            out_specs=(VMEM,) * (2 + len(extra)),
-            name="prepare_own" if first else "prepare_row",
-        )(near(source), *params)
-
-    basis, row_terms, mix = prepare(payload, True)
+    shapes = (pltpu.VMEM((depth, tiles * lanes), BF16), pltpu.VMEM((8 * tiles, lanes), F32))
+    basis, row_terms, mix, terms = pl.pallas_call(
+        functools.partial(prepare_kernel, walkers, rows),
+        out_shape=shapes + (pltpu.VMEM((lanes, lanes), BF16), pltpu.VMEM((3, lanes), F32)),
+        in_specs=[VMEM] * 4,
+        out_specs=(VMEM,) * 4,
+        name="prepare_own",
+    )(near(payload), *params)
     bases, row_sets = [basis], [row_terms]
     for source in bigs[1:]:
-        basis, row_terms = prepare(source, False)
+        basis, row_terms = pl.pallas_call(
+            functools.partial(prepare_row_kernel, walkers, rows),
+            out_shape=shapes,
+            in_specs=[VMEM] * 3,
+            out_specs=(VMEM,) * 2,
+            name="prepare_row",
+        )(near(source), params[0], near(terms))
         bases.append(basis)
         row_sets.append(row_terms)
     flat = 2 * width + 8

time: 28.7 us -> 28.7 us (level)
  no operation moved by 1% of the time
where the time goes in v3:
time: 28.7 us; the launch traced here: 28.6 us
  starting transfers between devices  14 us (49%)
  waiting for transfers between devices  8.33 us (29%)
  Pallas kernels  5.55 us (19%)
  between operations  0.69 us (2%)
    ppermute x11, starting transfers between devices, swap(): return lax.ppermute(x, axis, [(i, i ^ mask) for i in range(size)])  14 us
    ppermute x11, waiting for transfers between devices, swap(): return lax.ppermute(x, axis, [(i, i ^ mask) for i in range(size)])  8.33 us
    pallas_call x1, Pallas kernels, on_device(): pl.pallas_call(functools.partial(pair_kernel, walkers, width, rows, total...  2.03 us
    pallas_call x1, Pallas kernels, on_device(): pl.pallas_call(functools.partial(embed_kernel, total), out_shape=(pltpu.V...  1.07 us
    pallas_call x1, Pallas kernels, on_device(): pl.pallas_call(functools.partial(hidden_kernel, offsets), out_shape=jax.S...  0.96 us
    pallas_call x1, Pallas kernels, on_device(): pl.pallas_call(finish_kernel, out_shape=(jax.ShapeDtypeStruct((width, hid...  0.68 us
  transfers between devices with their start and end apart: 11, of which 7 were waited for; matrix products, arithmetic and copies ran while one was open for 0% of the time, Pallas kernels for 5%

profile of v3, /device:TPU:0, one launch (start us, length us, event | category | flops | bytes accessed | tf_op | source)
XLA Modules:
  0.0 28.6 jit_solution(8046437955199398136)
XLA Ops:
  0.6 1.1 %embed.1 = (f32[40,128]{1,0:T(8,128)S(1)}, f32[296,128]{1,0:T(8,128)S(1)}, bf16[32,256]{1,0:T(8,128)(2,1)S(1)}, f32[32,32]{1,0:T(8,128)S(1)}, f32[2,32]{1,0:T(2,128)S(1)}, /*index=5*/f32[1,32]{1,0:T(1,128)S(1)}) custom-call(bf16[4,16,256]{2,1,0:T(8,128)(2,1)} %hid.1, bf16[4,16,256]{2,1,0:T(8,128)(2,1)} %cot.1, f32[3,4,16]{2,1,0:T(4,128)} %bitcast.7, ...), custom_call_target="tpu_custom_call" | custom-call | tf_op jit(solution)/shard_map/embed/pallas_call | solution.py:383
  1.7 3.1 %collective-permute-start.3 = (f32[296,128]{1,0:T(8,128)S(1)}, f32[296,128]{1,0:T(8,128)S(1)}, u32[]{:S(2)}, u32[]{:S(2)}) collective-permute-start(f32[296,128]{1,0:T(8,128)S(1)} %get-tuple-element.25.refs_2_), channel_id=1, source_target_pairs={{0,4},{2,6},{4,0},{6,2},{8,12},{10,14},{12,8},{14,10},{1,5},{3,7},... | collective-permute-start | bytes 454664 | tf_op jit(solution)/shard_map/ppermute | solution.py:345
  4.8 3.5 %collective-permute-start.2 = (f32[40,128]{1,0:T(8,128)S(1)}, f32[40,128]{1,0:T(8,128)S(1)}, u32[]{:S(2)}, u32[]{:S(2)}) collective-permute-start(f32[40,128]{1,0:T(8,128)S(1)} %get-tuple-element.24.own), channel_id=1, source_target_pairs={{0,10},{2,8},{4,14},{6,12},{8,2},{10,0},{12,6},{14,4},{1,11},{3,9}... | collective-permute-start | bytes 61448 | tf_op jit(solution)/shard_map/ppermute | solution.py:345
  8.4 0.3 %collective-permute-start.1 = (f32[40,128]{1,0:T(8,128)S(1)}, f32[40,128]{1,0:T(8,128)S(1)}, u32[]{:S(2)}, u32[]{:S(2)}) collective-permute-start(f32[40,128]{1,0:T(8,128)S(1)} %get-tuple-element.24.own), channel_id=1, source_target_pairs={{0,8},{2,10},{4,12},{6,14},{8,0},{10,2},{12,4},{14,6},{1,9},{3,11}... | collective-permute-start | bytes 61448 | tf_op jit(solution)/shard_map/ppermute | solution.py:345
  8.7 0.5 %collective-permute-start = (f32[40,128]{1,0:T(8,128)S(1)}, f32[40,128]{1,0:T(8,128)S(1)}, u32[]{:S(2)}, u32[]{:S(2)}) collective-permute-start(f32[40,128]{1,0:T(8,128)S(1)} %get-tuple-element.24.own), channel_id=1, source_target_pairs={{0,2},{2,0},{4,6},{6,4},{8,10},{10,8},{12,14},{14,12},{1,3},{3,1},... | collective-permute-start | bytes 61448 | tf_op jit(solution)/shard_map/ppermute | solution.py:345
  9.2 0.4 %prepare_own.1 = (bf16[192,2048]{1,0:T(8,128)(2,1)S(1)}, f32[64,256]{1,0:T(8,128)S(1)}, bf16[256,256]{1,0:T(8,128)(2,1)S(1)}, f32[3,256]{1,0:T(4,128)S(1)}) custom-call(f32[40,128]{1,0:T(8,128)S(1)} %get-tuple-element.24.own, f32[32,32]{1,0:T(8,128)S(1)} %get-tuple-element.26.w_pair, f32[2,32]{1,0:T(2,128)S(1)} %get-tuple-element.27.spin_bias, ...), custom_call_target="tpu_custom_call" | custom-call | tf_op jit(solution)/shard_map/prepare_own/pallas_call | solution.py:417
  9.6 0.8 %collective-permute-done.2 = f32[40,128]{1,0:T(8,128)S(1)} collective-permute-done((f32[40,128]{1,0:T(8,128)S(1)}, f32[40,128]{1,0:T(8,128)S(1)}, u32[]{:S(2)}, u32[]{:S(2)}) %collective-permute-start.2) | collective-permute-done | bytes 20512 | tf_op jit(solution)/shard_map/ppermute | solution.py:345
  10.4 2.7 %collective-permute-done.1 = f32[40,128]{1,0:T(8,128)S(1)} collective-permute-done((f32[40,128]{1,0:T(8,128)S(1)}, f32[40,128]{1,0:T(8,128)S(1)}, u32[]{:S(2)}, u32[]{:S(2)}) %collective-permute-start.1) | collective-permute-done | bytes 20512 | tf_op jit(solution)/shard_map/ppermute | solution.py:345
  13.2 0.0 collective-permute-done
  13.2 0.0 collective-permute-done.3.own.refs_3_
  13.2 0.4 %prepare_row.1 = (bf16[192,2048]{1,0:T(8,128)(2,1)S(1)}, f32[64,256]{1,0:T(8,128)S(1)}) custom-call(f32[296,128]{1,0:T(8,128)S(1)} %collective-permute-done.3.own.refs_3_, f32[32,32]{1,0:T(8,128)S(1)} %get-tuple-element.26.w_pair, f32[3,256]{1,0:T(4,128)S(1)} %get-tuple-element.30.terms), custom_call_target="tpu_custom_call" | custom-call | tf_op jit(solution)/shard_map/prepare_row/pallas_call | solution.py:426
  13.6 2.0 %pairs.1 = (f32[64,128]{1,0:T(8,128)S(1)}, f32[88,128]{1,0:T(8,128)S(1)}, f32[72,128]{1,0:T(8,128)S(1)}) custom-call(s32[1]{0:T(128)} %bitcast.refs_0_.side, f32[160,128]{1,0:T(8,128)S(1)} %pad_maximum_fusion.refs_1_, f32[296,128]{1,0:T(8,128)S(1)} %get-tuple-element.25.refs_2_, f32[296,128]{1,0:T(8,128)S(1)} %collective-permute-done.3.own.refs_3_, ...), custom_call_target="tpu_custom_call" | custom-call | tf_op jit(solution)/shard_map/pairs/pallas_call | solution.py:439
  15.6 0.4 %collective-permute-start.4 = (f32[88,128]{1,0:T(8,128)S(1)}, f32[88,128]{1,0:T(8,128)S(1)}, u32[]{:S(2)}, u32[]{:S(2)}) collective-permute-start(f32[88,128]{1,0:T(8,128)S(1)} %get-tuple-element.37), channel_id=1, source_target_pairs={{0,4},{2,6},{4,0},{6,2},{8,12},{10,14},{12,8},{14,10},{1,5},{3,7},... | collective-permute-start | bytes 135176 | tf_op jit(solution)/shard_map/ppermute | solution.py:345
  16.0 0.0 collective-permute-start.6
  16.0 1.8 %collective-permute-start.5 = (f32[72,128]{1,0:T(8,128)S(1)}, f32[72,128]{1,0:T(8,128)S(1)}, u32[]{:S(2)}, u32[]{:S(2)}) collective-permute-start(f32[72,128]{1,0:T(8,128)S(1)} %get-tuple-element.38), channel_id=1, source_target_pairs={{0,1},{1,0},{2,3},{3,2},{4,5},{5,4},{6,7},{7,6},{8,9},{9,8},{10,11... | collective-permute-start | bytes 110600 | tf_op jit(solution)/shard_map/ppermute | solution.py:345
  17.8 1.8 %collective-permute-done.6 = f32[72,128]{1,0:T(8,128)S(1)} collective-permute-done((f32[72,128]{1,0:T(8,128)S(1)}, f32[72,128]{1,0:T(8,128)S(1)}, u32[]{:S(2)}, u32[]{:S(2)}) %collective-permute-start.6) | collective-permute-done | bytes 36896 | tf_op jit(solution)/shard_map/ppermute | solution.py:345
  19.5 0.0 collective-permute-done.5
  19.5 0.3 %collective-permute-done.4.refs_0_ = f32[88,128]{1,0:T(8,128)S(1)} collective-permute-done((f32[88,128]{1,0:T(8,128)S(1)}, f32[88,128]{1,0:T(8,128)S(1)}, u32[]{:S(2)}, u32[]{:S(2)}) %collective-permute-start.4) | collective-permute-done | bytes 45088 | tf_op jit(solution)/shard_map/ppermute | solution.py:345
  19.9 1.8 %collective-permute-start.9 = (f32[72,128]{1,0:T(8,128)S(1)}, f32[72,128]{1,0:T(8,128)S(1)}, u32[]{:S(2)}, u32[]{:S(2)}) collective-permute-start(f32[72,128]{1,0:T(8,128)S(1)} %fusion), channel_id=1, source_target_pairs={{0,11},{1,10},{2,9},{3,8},{4,15},{5,14},{6,13},{7,12},{8,3},{9,2},... | collective-permute-start | bytes 110600 | tf_op jit(solution)/shard_map/ppermute | solution.py:345
  21.7 0.8 %collective-permute-start.8 = (f32[72,128]{1,0:T(8,128)S(1)}, f32[72,128]{1,0:T(8,128)S(1)}, u32[]{:S(2)}, u32[]{:S(2)}) collective-permute-start(f32[72,128]{1,0:T(8,128)S(1)} %fusion), channel_id=1, source_target_pairs={{0,9},{1,8},{2,11},{3,10},{4,13},{5,12},{6,15},{7,14},{8,1},{9,0},... | collective-permute-start | bytes 110600 | tf_op jit(solution)/shard_map/ppermute | solution.py:345
  22.5 1.5 %collective-permute-start.7 = (f32[72,128]{1,0:T(8,128)S(1)}, f32[72,128]{1,0:T(8,128)S(1)}, u32[]{:S(2)}, u32[]{:S(2)}) collective-permute-start(f32[72,128]{1,0:T(8,128)S(1)} %fusion), channel_id=1, source_target_pairs={{0,2},{1,3},{2,0},{3,1},{4,6},{5,7},{6,4},{7,5},{8,10},{9,11},{10,... | collective-permute-start | bytes 110600 | tf_op jit(solution)/shard_map/ppermute | solution.py:345
  24.0 2.1 %collective-permute-done.9 = f32[72,128]{1,0:T(8,128)S(1)} collective-permute-done((f32[72,128]{1,0:T(8,128)S(1)}, f32[72,128]{1,0:T(8,128)S(1)}, u32[]{:S(2)}, u32[]{:S(2)}) %collective-permute-start.9) | collective-permute-done | bytes 36896 | tf_op jit(solution)/shard_map/ppermute | solution.py:345
  26.2 0.0 collective-permute-done.8
  26.2 0.4 %collective-permute-done.7 = f32[72,128]{1,0:T(8,128)S(1)} collective-permute-done((f32[72,128]{1,0:T(8,128)S(1)}, f32[72,128]{1,0:T(8,128)S(1)}, u32[]{:S(2)}, u32[]{:S(2)}) %collective-permute-start.7) | collective-permute-done | bytes 36896 | tf_op jit(solution)/shard_map/ppermute | solution.py:345
  26.6 0.1 collective-permute-start.10
  26.7 1.0 %hidden_grad.1 = bf16[4,16,256]{2,1,0:T(8,128)(2,1)} custom-call(f32[64,128]{1,0:T(8,128)S(1)} %get-tuple-element.35.sens, bf16[32,256]{1,0:T(8,128)(2,1)S(1)} %get-tuple-element.36.w_in, f32[88,128]{1,0:T(8,128)S(1)} %collective-permute-done.4.refs_0_), custom_call_target="tpu_custom_call" | custom-call | tf_op jit(solution)/shard_map/hidden_grad/pallas_call | solution.py:455
  27.7 0.2 collective-permute-done.10.other
  27.9 0.7 %finish.1 = (f32[32,256]{1,0:T(8,128)}, f32[32,32]{1,0:T(8,128)}, f32[2,32]{1,0:T(2,128)}, f32[32,256]{1,0:T(8,128)}) custom-call(s32[1]{0:T(128)} %bitcast.refs_0_.side, f32[72,128]{1,0:T(8,128)S(1)} %add_add_fusion.mine, f32[72,128]{1,0:T(8,128)S(1)} %collective-permute-done.10.other), custom_call_target="tpu_custom_call" | custom-call | tf_op jit(solution)/shard_map/finish/pallas_call | solution.py:470
  (3 shorter events, 0.0 us)
Async XLA Ops:
  1.7 11.5 %collective-permute-start.3 = (f32[296,128]{1,0:T(8,128)S(1)}, f32[296,128]{1,0:T(8,128)S(1)}, u32[]{:S(2)}, u32[]{:S(2)}) collective-permute-start(f32[296,128]{1,0:T(8,128)S(1)} %get-tuple-element.25.refs_2_), channel_id=1, source_target_pairs={{0,4},{2,6},{4,0},{6,2},{8,12},{10,14},{12,8},{14,10},{1,5},{3,7},... | collective-permute-start | bytes 454664 | tf_op jit(solution)/shard_map/ppermute | solution.py:345
  4.8 5.6 %collective-permute-start.2 = (f32[40,128]{1,0:T(8,128)S(1)}, f32[40,128]{1,0:T(8,128)S(1)}, u32[]{:S(2)}, u32[]{:S(2)}) collective-permute-start(f32[40,128]{1,0:T(8,128)S(1)} %get-tuple-element.24.own), channel_id=1, source_target_pairs={{0,10},{2,8},{4,14},{6,12},{8,2},{10,0},{12,6},{14,4},{1,11},{3,9}... | collective-permute-start | bytes 61448 | tf_op jit(solution)/shard_map/ppermute | solution.py:345
  8.4 4.8 %collective-permute-start.1 = (f32[40,128]{1,0:T(8,128)S(1)}, f32[40,128]{1,0:T(8,128)S(1)}, u32[]{:S(2)}, u32[]{:S(2)}) collective-permute-start(f32[40,128]{1,0:T(8,128)S(1)} %get-tuple-element.24.own), channel_id=1, source_target_pairs={{0,8},{2,10},{4,12},{6,14},{8,0},{10,2},{12,4},{14,6},{1,9},{3,11}... | collective-permute-start | bytes 61448 | tf_op jit(solution)/shard_map/ppermute | solution.py:345
  8.7 4.5 %collective-permute-start = (f32[40,128]{1,0:T(8,128)S(1)}, f32[40,128]{1,0:T(8,128)S(1)}, u32[]{:S(2)}, u32[]{:S(2)}) collective-permute-start(f32[40,128]{1,0:T(8,128)S(1)} %get-tuple-element.24.own), channel_id=1, source_target_pairs={{0,2},{2,0},{4,6},{6,4},{8,10},{10,8},{12,14},{14,12},{1,3},{3,1},... | collective-permute-start | bytes 61448 | tf_op jit(solution)/shard_map/ppermute | solution.py:345
  15.6 4.2 %collective-permute-start.4 = (f32[88,128]{1,0:T(8,128)S(1)}, f32[88,128]{1,0:T(8,128)S(1)}, u32[]{:S(2)}, u32[]{:S(2)}) collective-permute-start(f32[88,128]{1,0:T(8,128)S(1)} %get-tuple-element.37), channel_id=1, source_target_pairs={{0,4},{2,6},{4,0},{6,2},{8,12},{10,14},{12,8},{14,10},{1,5},{3,7},... | collective-permute-start | bytes 135176 | tf_op jit(solution)/shard_map/ppermute | solution.py:345
  16.0 3.6 %collective-permute-start.6 = (f32[72,128]{1,0:T(8,128)S(1)}, f32[72,128]{1,0:T(8,128)S(1)}, u32[]{:S(2)}, u32[]{:S(2)}) collective-permute-start(f32[72,128]{1,0:T(8,128)S(1)} %get-tuple-element.38), channel_id=1, source_target_pairs={{0,5},{1,4},{2,7},{3,6},{4,1},{5,0},{6,3},{7,2},{8,13},{9,12},{10,... | collective-permute-start | bytes 110600 | tf_op jit(solution)/shard_map/ppermute | solution.py:345
  16.0 3.6 %collective-permute-start.5 = (f32[72,128]{1,0:T(8,128)S(1)}, f32[72,128]{1,0:T(8,128)S(1)}, u32[]{:S(2)}, u32[]{:S(2)}) collective-permute-start(f32[72,128]{1,0:T(8,128)S(1)} %get-tuple-element.38), channel_id=1, source_target_pairs={{0,1},{1,0},{2,3},{3,2},{4,5},{5,4},{6,7},{7,6},{8,9},{9,8},{10,11... | collective-permute-start | bytes 110600 | tf_op jit(solution)/shard_map/ppermute | solution.py:345
  19.9 6.3 %collective-permute-start.9 = (f32[72,128]{1,0:T(8,128)S(1)}, f32[72,128]{1,0:T(8,128)S(1)}, u32[]{:S(2)}, u32[]{:S(2)}) collective-permute-start(f32[72,128]{1,0:T(8,128)S(1)} %fusion), channel_id=1, source_target_pairs={{0,11},{1,10},{2,9},{3,8},{4,15},{5,14},{6,13},{7,12},{8,3},{9,2},... | collective-permute-start | bytes 110600 | tf_op jit(solution)/shard_map/ppermute | solution.py:345
  21.7 4.5 %collective-permute-start.8 = (f32[72,128]{1,0:T(8,128)S(1)}, f32[72,128]{1,0:T(8,128)S(1)}, u32[]{:S(2)}, u32[]{:S(2)}) collective-permute-start(f32[72,128]{1,0:T(8,128)S(1)} %fusion), channel_id=1, source_target_pairs={{0,9},{1,8},{2,11},{3,10},{4,13},{5,12},{6,15},{7,14},{8,1},{9,0},... | collective-permute-start | bytes 110600 | tf_op jit(solution)/shard_map/ppermute | solution.py:345
  22.5 4.1 %collective-permute-start.7 = (f32[72,128]{1,0:T(8,128)S(1)}, f32[72,128]{1,0:T(8,128)S(1)}, u32[]{:S(2)}, u32[]{:S(2)}) collective-permute-start(f32[72,128]{1,0:T(8,128)S(1)} %fusion), channel_id=1, source_target_pairs={{0,2},{1,3},{2,0},{3,1},{4,6},{5,7},{6,4},{7,5},{8,10},{9,11},{10,... | collective-permute-start | bytes 110600 | tf_op jit(solution)/shard_map/ppermute | solution.py:345
  26.6 1.3 %collective-permute-start.10 = (f32[72,128]{1,0:T(8,128)S(1)}, f32[72,128]{1,0:T(8,128)S(1)}, u32[]{:S(2)}, u32[]{:S(2)}) collective-permute-start(f32[72,128]{1,0:T(8,128)S(1)} %add_add_fusion.mine), channel_id=1, source_target_pairs={{0,1},{1,0},{2,3},{3,2},{4,5},{5,4},{6,7},{7,6},{8,9},{9,8},{10,11... | collective-permute-start | bytes 110600 | tf_op jit(solution)/shard_map/ppermute | solution.py:345

commit v4 on v3

--- a/solution.py
+++ b/solution.py
@@ -132,7 +132,11 @@
     groups, parts, spins = [], [], []
     for h in range(rows // PACK):
         group = flag(iota((rows, lanes), 1) // width + PACK * h == iota((rows, lanes), 0))
-        cols = dot_exact(feat, group, ((0,), (0,)))
+        cols = dot(
+            jnp.concatenate(thirds(feat), axis=0),
+            jnp.concatenate([group] * 3, axis=0).astype(BF16),
+            ((0,), (0,)),
+        )
         spins.append(cols[spin_at : spin_at + 1])
         groups.append(group)
         parts.append(thirds(jnp.where(feat_row == spin_at + 1, -3.0, cols) * rate_row))

time: 28.7 us -> 28.7 us (level)
  no operation moved by 1% of the time
where the time goes in v4:
time: 28.7 us; the launch traced here: 28.5 us
  starting transfers between devices  14 us (49%)
  waiting for transfers between devices  8.36 us (29%)
  Pallas kernels  5.44 us (19%)
  between operations  0.69 us (2%)
    ppermute x11, starting transfers between devices, swap(): return lax.ppermute(x, axis, [(i, i ^ mask) for i in range(size)])  14 us
    ppermute x11, waiting for transfers between devices, swap(): return lax.ppermute(x, axis, [(i, i ^ mask) for i in range(size)])  8.36 us
    pallas_call x1, Pallas kernels, on_device(): pl.pallas_call(functools.partial(pair_kernel, walkers, width, rows, total...  2.03 us
    pallas_call x1, Pallas kernels, on_device(): pl.pallas_call(functools.partial(embed_kernel, total), out_shape=(pltpu.V...  1.07 us
    pallas_call x1, Pallas kernels, on_device(): pl.pallas_call(functools.partial(hidden_kernel, offsets), out_shape=jax.S...  0.96 us
    pallas_call x1, Pallas kernels, on_device(): pl.pallas_call(finish_kernel, out_shape=(jax.ShapeDtypeStruct((width, hid...  0.68 us
  transfers between devices with their start and end apart: 11, of which 7 were waited for; matrix products, arithmetic and copies ran while one was open for 0% of the time, Pallas kernels for 5%

profile of v4, /device:TPU:0, one launch (start us, length us, event | category | flops | bytes accessed | tf_op | source)
XLA Modules:
  0.0 28.5 jit_solution(11771152057586350136)
XLA Ops:
  0.6 1.1 %embed.1 = (f32[40,128]{1,0:T(8,128)S(1)}, f32[296,128]{1,0:T(8,128)S(1)}, bf16[32,256]{1,0:T(8,128)(2,1)S(1)}, f32[32,32]{1,0:T(8,128)S(1)}, f32[2,32]{1,0:T(2,128)S(1)}, /*index=5*/f32[1,32]{1,0:T(1,128)S(1)}) custom-call(bf16[4,16,256]{2,1,0:T(8,128)(2,1)} %hid.1, bf16[4,16,256]{2,1,0:T(8,128)(2,1)} %cot.1, f32[3,4,16]{2,1,0:T(4,128)} %bitcast.7, ...), custom_call_target="tpu_custom_call" | custom-call | tf_op jit(solution)/shard_map/embed/pallas_call | solution.py:387
  1.7 3.1 %collective-permute-start.3 = (f32[296,128]{1,0:T(8,128)S(1)}, f32[296,128]{1,0:T(8,128)S(1)}, u32[]{:S(2)}, u32[]{:S(2)}) collective-permute-start(f32[296,128]{1,0:T(8,128)S(1)} %get-tuple-element.25.refs_2_), channel_id=1, source_target_pairs={{0,4},{2,6},{4,0},{6,2},{8,12},{10,14},{12,8},{14,10},{1,5},{3,7},... | collective-permute-start | bytes 454664 | tf_op jit(solution)/shard_map/ppermute | solution.py:349
  4.8 3.5 %collective-permute-start.2 = (f32[40,128]{1,0:T(8,128)S(1)}, f32[40,128]{1,0:T(8,128)S(1)}, u32[]{:S(2)}, u32[]{:S(2)}) collective-permute-start(f32[40,128]{1,0:T(8,128)S(1)} %get-tuple-element.24.own), channel_id=1, source_target_pairs={{0,10},{2,8},{4,14},{6,12},{8,2},{10,0},{12,6},{14,4},{1,11},{3,9}... | collective-permute-start | bytes 61448 | tf_op jit(solution)/shard_map/ppermute | solution.py:349
  8.4 0.3 %collective-permute-start.1 = (f32[40,128]{1,0:T(8,128)S(1)}, f32[40,128]{1,0:T(8,128)S(1)}, u32[]{:S(2)}, u32[]{:S(2)}) collective-permute-start(f32[40,128]{1,0:T(8,128)S(1)} %get-tuple-element.24.own), channel_id=1, source_target_pairs={{0,8},{2,10},{4,12},{6,14},{8,0},{10,2},{12,4},{14,6},{1,9},{3,11}... | collective-permute-start | bytes 61448 | tf_op jit(solution)/shard_map/ppermute | solution.py:349
  8.7 0.5 %collective-permute-start = (f32[40,128]{1,0:T(8,128)S(1)}, f32[40,128]{1,0:T(8,128)S(1)}, u32[]{:S(2)}, u32[]{:S(2)}) collective-permute-start(f32[40,128]{1,0:T(8,128)S(1)} %get-tuple-element.24.own), channel_id=1, source_target_pairs={{0,2},{2,0},{4,6},{6,4},{8,10},{10,8},{12,14},{14,12},{1,3},{3,1},... | collective-permute-start | bytes 61448 | tf_op jit(solution)/shard_map/ppermute | solution.py:349
  9.2 0.4 %prepare_own.1 = (bf16[192,2048]{1,0:T(8,128)(2,1)S(1)}, f32[64,256]{1,0:T(8,128)S(1)}, bf16[256,256]{1,0:T(8,128)(2,1)S(1)}, f32[3,256]{1,0:T(4,128)S(1)}) custom-call(f32[40,128]{1,0:T(8,128)S(1)} %get-tuple-element.24.own, f32[32,32]{1,0:T(8,128)S(1)} %get-tuple-element.26.w_pair, f32[2,32]{1,0:T(2,128)S(1)} %get-tuple-element.27.spin_bias, ...), custom_call_target="tpu_custom_call" | custom-call | tf_op jit(solution)/shard_map/prepare_own/pallas_call | solution.py:421
  9.6 0.8 %collective-permute-done.2 = f32[40,128]{1,0:T(8,128)S(1)} collective-permute-done((f32[40,128]{1,0:T(8,128)S(1)}, f32[40,128]{1,0:T(8,128)S(1)}, u32[]{:S(2)}, u32[]{:S(2)}) %collective-permute-start.2) | collective-permute-done | bytes 20512 | tf_op jit(solution)/shard_map/ppermute | solution.py:349
  10.4 2.7 %collective-permute-done.1 = f32[40,128]{1,0:T(8,128)S(1)} collective-permute-done((f32[40,128]{1,0:T(8,128)S(1)}, f32[40,128]{1,0:T(8,128)S(1)}, u32[]{:S(2)}, u32[]{:S(2)}) %collective-permute-start.1) | collective-permute-done | bytes 20512 | tf_op jit(solution)/shard_map/ppermute | solution.py:349
  13.2 0.0 collective-permute-done
  13.2 0.0 collective-permute-done.3.own.refs_3_
  13.2 0.3 %prepare_row.1 = (bf16[192,2048]{1,0:T(8,128)(2,1)S(1)}, f32[64,256]{1,0:T(8,128)S(1)}) custom-call(f32[296,128]{1,0:T(8,128)S(1)} %collective-permute-done.3.own.refs_3_, f32[32,32]{1,0:T(8,128)S(1)} %get-tuple-element.26.w_pair, f32[3,256]{1,0:T(4,128)S(1)} %get-tuple-element.30.terms), custom_call_target="tpu_custom_call" | custom-call | tf_op jit(solution)/shard_map/prepare_row/pallas_call | solution.py:430
  13.5 2.0 %pairs.1 = (f32[64,128]{1,0:T(8,128)S(1)}, f32[88,128]{1,0:T(8,128)S(1)}, f32[72,128]{1,0:T(8,128)S(1)}) custom-call(s32[1]{0:T(128)} %bitcast.refs_0_.side, f32[160,128]{1,0:T(8,128)S(1)} %pad_maximum_fusion.refs_1_, f32[296,128]{1,0:T(8,128)S(1)} %get-tuple-element.25.refs_2_, f32[296,128]{1,0:T(8,128)S(1)} %collective-permute-done.3.own.refs_3_, ...), custom_call_target="tpu_custom_call" | custom-call | tf_op jit(solution)/shard_map/pairs/pallas_call | solution.py:443
  15.6 0.4 %collective-permute-start.4 = (f32[88,128]{1,0:T(8,128)S(1)}, f32[88,128]{1,0:T(8,128)S(1)}, u32[]{:S(2)}, u32[]{:S(2)}) collective-permute-start(f32[88,128]{1,0:T(8,128)S(1)} %get-tuple-element.37), channel_id=1, source_target_pairs={{0,4},{2,6},{4,0},{6,2},{8,12},{10,14},{12,8},{14,10},{1,5},{3,7},... | collective-permute-start | bytes 135176 | tf_op jit(solution)/shard_map/ppermute | solution.py:349
  15.9 0.0 collective-permute-start.6
  15.9 1.8 %collective-permute-start.5 = (f32[72,128]{1,0:T(8,128)S(1)}, f32[72,128]{1,0:T(8,128)S(1)}, u32[]{:S(2)}, u32[]{:S(2)}) collective-permute-start(f32[72,128]{1,0:T(8,128)S(1)} %get-tuple-element.38), channel_id=1, source_target_pairs={{0,1},{1,0},{2,3},{3,2},{4,5},{5,4},{6,7},{7,6},{8,9},{9,8},{10,11... | collective-permute-start | bytes 110600 | tf_op jit(solution)/shard_map/ppermute | solution.py:349
  17.7 1.8 %collective-permute-done.6 = f32[72,128]{1,0:T(8,128)S(1)} collective-permute-done((f32[72,128]{1,0:T(8,128)S(1)}, f32[72,128]{1,0:T(8,128)S(1)}, u32[]{:S(2)}, u32[]{:S(2)}) %collective-permute-start.6) | collective-permute-done | bytes 36896 | tf_op jit(solution)/shard_map/ppermute | solution.py:349
  19.5 0.0 collective-permute-done.5
  19.5 0.3 %collective-permute-done.4.refs_0_ = f32[88,128]{1,0:T(8,128)S(1)} collective-permute-done((f32[88,128]{1,0:T(8,128)S(1)}, f32[88,128]{1,0:T(8,128)S(1)}, u32[]{:S(2)}, u32[]{:S(2)}) %collective-permute-start.4) | collective-permute-done | bytes 45088 | tf_op jit(solution)/shard_map/ppermute | solution.py:349
  19.8 1.8 %collective-permute-start.9 = (f32[72,128]{1,0:T(8,128)S(1)}, f32[72,128]{1,0:T(8,128)S(1)}, u32[]{:S(2)}, u32[]{:S(2)}) collective-permute-start(f32[72,128]{1,0:T(8,128)S(1)} %fusion), channel_id=1, source_target_pairs={{0,11},{1,10},{2,9},{3,8},{4,15},{5,14},{6,13},{7,12},{8,3},{9,2},... | collective-permute-start | bytes 110600 | tf_op jit(solution)/shard_map/ppermute | solution.py:349
  21.6 0.8 %collective-permute-start.8 = (f32[72,128]{1,0:T(8,128)S(1)}, f32[72,128]{1,0:T(8,128)S(1)}, u32[]{:S(2)}, u32[]{:S(2)}) collective-permute-start(f32[72,128]{1,0:T(8,128)S(1)} %fusion), channel_id=1, source_target_pairs={{0,9},{1,8},{2,11},{3,10},{4,13},{5,12},{6,15},{7,14},{8,1},{9,0},... | collective-permute-start | bytes 110600 | tf_op jit(solution)/shard_map/ppermute | solution.py:349
  22.5 1.5 %collective-permute-start.7 = (f32[72,128]{1,0:T(8,128)S(1)}, f32[72,128]{1,0:T(8,128)S(1)}, u32[]{:S(2)}, u32[]{:S(2)}) collective-permute-start(f32[72,128]{1,0:T(8,128)S(1)} %fusion), channel_id=1, source_target_pairs={{0,2},{1,3},{2,0},{3,1},{4,6},{5,7},{6,4},{7,5},{8,10},{9,11},{10,... | collective-permute-start | bytes 110600 | tf_op jit(solution)/shard_map/ppermute | solution.py:349
  24.0 2.1 %collective-permute-done.9 = f32[72,128]{1,0:T(8,128)S(1)} collective-permute-done((f32[72,128]{1,0:T(8,128)S(1)}, f32[72,128]{1,0:T(8,128)S(1)}, u32[]{:S(2)}, u32[]{:S(2)}) %collective-permute-start.9) | collective-permute-done | bytes 36896 | tf_op jit(solution)/shard_map/ppermute | solution.py:349
  26.1 0.0 collective-permute-done.8
  26.1 0.4 %collective-permute-done.7 = f32[72,128]{1,0:T(8,128)S(1)} collective-permute-done((f32[72,128]{1,0:T(8,128)S(1)}, f32[72,128]{1,0:T(8,128)S(1)}, u32[]{:S(2)}, u32[]{:S(2)}) %collective-permute-start.7) | collective-permute-done | bytes 36896 | tf_op jit(solution)/shard_map/ppermute | solution.py:349
  26.5 0.1 collective-permute-start.10
  26.7 1.0 %hidden_grad.1 = bf16[4,16,256]{2,1,0:T(8,128)(2,1)} custom-call(f32[64,128]{1,0:T(8,128)S(1)} %get-tuple-element.35.sens, bf16[32,256]{1,0:T(8,128)(2,1)S(1)} %get-tuple-element.36.w_in, f32[88,128]{1,0:T(8,128)S(1)} %collective-permute-done.4.refs_0_), custom_call_target="tpu_custom_call" | custom-call | tf_op jit(solution)/shard_map/hidden_grad/pallas_call | solution.py:459
  27.6 0.2 collective-permute-done.10.other
  27.8 0.7 %finish.1 = (f32[32,256]{1,0:T(8,128)}, f32[32,32]{1,0:T(8,128)}, f32[2,32]{1,0:T(2,128)}, f32[32,256]{1,0:T(8,128)}) custom-call(s32[1]{0:T(128)} %bitcast.refs_0_.side, f32[72,128]{1,0:T(8,128)S(1)} %add_add_fusion.mine, f32[72,128]{1,0:T(8,128)S(1)} %collective-permute-done.10.other), custom_call_target="tpu_custom_call" | custom-call | tf_op jit(solution)/shard_map/finish/pallas_call | solution.py:474
  (3 shorter events, 0.0 us)
Async XLA Ops:
  1.7 11.5 %collective-permute-start.3 = (f32[296,128]{1,0:T(8,128)S(1)}, f32[296,128]{1,0:T(8,128)S(1)}, u32[]{:S(2)}, u32[]{:S(2)}) collective-permute-start(f32[296,128]{1,0:T(8,128)S(1)} %get-tuple-element.25.refs_2_), channel_id=1, source_target_pairs={{0,4},{2,6},{4,0},{6,2},{8,12},{10,14},{12,8},{14,10},{1,5},{3,7},... | collective-permute-start | bytes 454664 | tf_op jit(solution)/shard_map/ppermute | solution.py:349
  4.8 5.6 %collective-permute-start.2 = (f32[40,128]{1,0:T(8,128)S(1)}, f32[40,128]{1,0:T(8,128)S(1)}, u32[]{:S(2)}, u32[]{:S(2)}) collective-permute-start(f32[40,128]{1,0:T(8,128)S(1)} %get-tuple-element.24.own), channel_id=1, source_target_pairs={{0,10},{2,8},{4,14},{6,12},{8,2},{10,0},{12,6},{14,4},{1,11},{3,9}... | collective-permute-start | bytes 61448 | tf_op jit(solution)/shard_map/ppermute | solution.py:349
  8.4 4.8 %collective-permute-start.1 = (f32[40,128]{1,0:T(8,128)S(1)}, f32[40,128]{1,0:T(8,128)S(1)}, u32[]{:S(2)}, u32[]{:S(2)}) collective-permute-start(f32[40,128]{1,0:T(8,128)S(1)} %get-tuple-element.24.own), channel_id=1, source_target_pairs={{0,8},{2,10},{4,12},{6,14},{8,0},{10,2},{12,4},{14,6},{1,9},{3,11}... | collective-permute-start | bytes 61448 | tf_op jit(solution)/shard_map/ppermute | solution.py:349
  8.7 4.5 %collective-permute-start = (f32[40,128]{1,0:T(8,128)S(1)}, f32[40,128]{1,0:T(8,128)S(1)}, u32[]{:S(2)}, u32[]{:S(2)}) collective-permute-start(f32[40,128]{1,0:T(8,128)S(1)} %get-tuple-element.24.own), channel_id=1, source_target_pairs={{0,2},{2,0},{4,6},{6,4},{8,10},{10,8},{12,14},{14,12},{1,3},{3,1},... | collective-permute-start | bytes 61448 | tf_op jit(solution)/shard_map/ppermute | solution.py:349
  15.6 4.2 %collective-permute-start.4 = (f32[88,128]{1,0:T(8,128)S(1)}, f32[88,128]{1,0:T(8,128)S(1)}, u32[]{:S(2)}, u32[]{:S(2)}) collective-permute-start(f32[88,128]{1,0:T(8,128)S(1)} %get-tuple-element.37), channel_id=1, source_target_pairs={{0,4},{2,6},{4,0},{6,2},{8,12},{10,14},{12,8},{14,10},{1,5},{3,7},... | collective-permute-start | bytes 135176 | tf_op jit(solution)/shard_map/ppermute | solution.py:349
  15.9 3.6 %collective-permute-start.6 = (f32[72,128]{1,0:T(8,128)S(1)}, f32[72,128]{1,0:T(8,128)S(1)}, u32[]{:S(2)}, u32[]{:S(2)}) collective-permute-start(f32[72,128]{1,0:T(8,128)S(1)} %get-tuple-element.38), channel_id=1, source_target_pairs={{0,5},{1,4},{2,7},{3,6},{4,1},{5,0},{6,3},{7,2},{8,13},{9,12},{10,... | collective-permute-start | bytes 110600 | tf_op jit(solution)/shard_map/ppermute | solution.py:349
  15.9 3.6 %collective-permute-start.5 = (f32[72,128]{1,0:T(8,128)S(1)}, f32[72,128]{1,0:T(8,128)S(1)}, u32[]{:S(2)}, u32[]{:S(2)}) collective-permute-start(f32[72,128]{1,0:T(8,128)S(1)} %get-tuple-element.38), channel_id=1, source_target_pairs={{0,1},{1,0},{2,3},{3,2},{4,5},{5,4},{6,7},{7,6},{8,9},{9,8},{10,11... | collective-permute-start | bytes 110600 | tf_op jit(solution)/shard_map/ppermute | solution.py:349
  19.8 6.3 %collective-permute-start.9 = (f32[72,128]{1,0:T(8,128)S(1)}, f32[72,128]{1,0:T(8,128)S(1)}, u32[]{:S(2)}, u32[]{:S(2)}) collective-permute-start(f32[72,128]{1,0:T(8,128)S(1)} %fusion), channel_id=1, source_target_pairs={{0,11},{1,10},{2,9},{3,8},{4,15},{5,14},{6,13},{7,12},{8,3},{9,2},... | collective-permute-start | bytes 110600 | tf_op jit(solution)/shard_map/ppermute | solution.py:349
  21.6 4.5 %collective-permute-start.8 = (f32[72,128]{1,0:T(8,128)S(1)}, f32[72,128]{1,0:T(8,128)S(1)}, u32[]{:S(2)}, u32[]{:S(2)}) collective-permute-start(f32[72,128]{1,0:T(8,128)S(1)} %fusion), channel_id=1, source_target_pairs={{0,9},{1,8},{2,11},{3,10},{4,13},{5,12},{6,15},{7,14},{8,1},{9,0},... | collective-permute-start | bytes 110600 | tf_op jit(solution)/shard_map/ppermute | solution.py:349
  22.5 4.1 %collective-permute-start.7 = (f32[72,128]{1,0:T(8,128)S(1)}, f32[72,128]{1,0:T(8,128)S(1)}, u32[]{:S(2)}, u32[]{:S(2)}) collective-permute-start(f32[72,128]{1,0:T(8,128)S(1)} %fusion), channel_id=1, source_target_pairs={{0,2},{1,3},{2,0},{3,1},{4,6},{5,7},{6,4},{7,5},{8,10},{9,11},{10,... | collective-permute-start | bytes 110600 | tf_op jit(solution)/shard_map/ppermute | solution.py:349
  26.5 1.3 %collective-permute-start.10 = (f32[72,128]{1,0:T(8,128)S(1)}, f32[72,128]{1,0:T(8,128)S(1)}, u32[]{:S(2)}, u32[]{:S(2)}) collective-permute-start(f32[72,128]{1,0:T(8,128)S(1)} %add_add_fusion.mine), channel_id=1, source_target_pairs={{0,1},{1,0},{2,3},{3,2},{4,5},{5,4},{6,7},{7,6},{8,9},{9,8},{10,11... | collective-permute-start | bytes 110600 | tf_op jit(solution)/shard_map/ppermute | solution.py:349
